TPU v7x, 32 devices: a whole 2x2x4 slice. The times are simulated.
32 devices in a mesh: ctx: 16 (over z, y, x), kvh: 2 (over core).
Axes of the slice: x: 2, y: 2, z: 4, core: 2. Of those that a mesh axis runs over, the one named last changes fastest.
Arguments:
- queries: bfloat16 [4096, 8192], P('ctx', 'kvh'), may hold values from -180 to 180
- keys: bfloat16 [4096, 1024], P('ctx', 'kvh'), may hold values from -6 to 6
- values: bfloat16 [4096, 1024], P('ctx', 'kvh'), may hold values from -6 to 6
- fwd_out: bfloat16 [4096, 8192], P('ctx', 'kvh'), may hold values from -4 to 4
- log_sum: float32 [64, 4096], P('kvh', 'ctx'), as said below
- out_grad: bfloat16 [4096, 8192], P('ctx', 'kvh'), may hold values from -6 to 6
- seg_ids: int32 [4096], replicated, may hold values from 0 to 3, as said below
- active: int32 [32, 16], P('ctx'), may hold values from 0 to 1, as said below
Outputs:
- grad_queries: bfloat16 [4096, 8192], P('ctx', 'kvh')
- grad_keys: bfloat16 [4096, 1024], P('ctx', 'kvh')
- grad_values: bfloat16 [4096, 1024], P('ctx', 'kvh')
Inputs may be any that keep to these rules, and one draw needn't show every extreme that they name: log_sum[h, t] is the logarithm of the sum over allowed u of exp(scores[h, t, u]) for the given queries and keys. `seg_ids`: document ids never fall along the sequence; every document has 1 to 2048 tokens, and one has exactly 2048. `active`: column 0 is 1 in every row; a row has 1 to 12 ones, and the last row exactly 12.
All inputs are finite; a program needn't handle non-finite values.
Results may differ from a plain program's by a relative error of at most 0.0049.
Values may be sent and summed in bfloat16 or wider, within the bound.
No kernel may reach another device: no remote copies, remote signals or barrier semaphores. Data moves between devices by JAX's collectives and lax.ppermute only.
A program may use at most 64 MiB of HBM per device.

v0:
```python
import functools

import jax
import jax.numpy as jnp
from jax import lax
from jax.experimental import pallas as pl
from jax.experimental.pallas import tpu as pltpu
from jax.sharding import PartitionSpec as P


D_HEAD = 128
BLK = 128
WINBLK = 16
EXTRA = 16
HALVES = 2
LOWEST = -1e30
LOG2E = 1.4426950408889634


NT = (((1,), (1,)), ((), ()))
TN = (((0,), (0,)), ((), ()))
F32, BF16 = jnp.float32, jnp.bfloat16
VMEM = pl.BlockSpec(memory_space=pltpu.VMEM)
SMEM = pl.BlockSpec(memory_space=pltpu.SMEM)
HBM = pl.BlockSpec(memory_space=pltpu.HBM)
ANY = pl.BlockSpec(memory_space=pl.ANY)
LARGE = pltpu.CompilerParams(vmem_limit_bytes=67043328)
SMALL = pltpu.CompilerParams(vmem_limit_bytes=16 << 20)


def kv_pack_kernel(groups, me_ref, key_ref, value_ref, active_ref, *outs):
    tokens = key_ref.shape[0]
    flags = active_ref[...].astype(F32).astype(BF16)
    for mask in range(groups):
        at = pl.ds(pl.multiple_of((me_ref[0] ^ mask) * D_HEAD, D_HEAD), D_HEAD)
        outs[mask][0:tokens, 0:D_HEAD] = key_ref[:, at]
        outs[mask][0:tokens, D_HEAD : 2 * D_HEAD] = value_ref[:, at]
        outs[mask][tokens : tokens + EXTRA, :] = jnp.zeros((EXTRA, 2 * D_HEAD), BF16)
        outs[mask][tokens : tokens + flags.shape[0], 0 : flags.shape[1]] = flags


def pack_kv(groups, me, keys, values, active):
    shape = jax.ShapeDtypeStruct((keys.shape[0] + EXTRA, 2 * D_HEAD), keys.dtype)
    return pl.pallas_call(
        functools.partial(kv_pack_kernel, groups),
        out_shape=[shape] * groups,
        in_specs=[SMEM] + [VMEM] * 3,
        out_specs=[VMEM] * groups,
        compiler_params=LARGE,
    )(me.reshape(1), keys, values, active)


def split_three(value):
    high = value.astype(BF16)
    rest = value - high.astype(F32)
    middle = rest.astype(BF16)
    return high, middle, (rest - middle.astype(F32)).astype(BF16)


def pair_pack_kernel(heads, group_ref, query_ref, grad_ref, fwd_ref, log_ref, out_ref):
    out_ref[0, 0:BLK, :] = query_ref[...]
    out_ref[0, BLK : 2 * BLK, :] = grad_ref[...]
    ones = jnp.ones((8, 2 * D_HEAD), BF16)
    rows = []
    for head in range(heads):
        cols = pl.ds(head * D_HEAD, D_HEAD)
        product = grad_ref[:, cols].astype(F32) * fwd_ref[:, cols].astype(F32)
        high = product.astype(BF16)
        low = (product - high.astype(F32)).astype(BF16)
        both = jnp.concatenate([high, low], axis=1)
        rows.append(lax.dot_general(ones, both, NT, preferred_element_type=F32)[0:1, :])
    pieces = split_three(log_ref[...]) + split_three(jnp.concatenate(rows, axis=0))
    blank = jnp.zeros((heads, heads * D_HEAD - len(pieces) * BLK), BF16)
    out_ref[0, 2 * BLK : 2 * BLK + heads, :] = jnp.concatenate(pieces + (blank,), axis=1)


def pack_pair(group, heads, queries, out_grad, fwd_out, log_sum):
    tokens = queries.shape[0]
    span = heads * D_HEAD
    spec = pl.BlockSpec((BLK, span), lambda i, g: (i, g[0]))
    return pl.pallas_call(
        functools.partial(pair_pack_kernel, heads),
        out_shape=jax.ShapeDtypeStruct((tokens // BLK, 2 * BLK + heads, span), queries.dtype),
        grid_spec=pltpu.PrefetchScalarGridSpec(
            num_scalar_prefetch=1,
            grid=(tokens // BLK,),
            in_specs=[spec, spec, spec, pl.BlockSpec((heads, BLK), lambda i, g: (g[0], i))],
            out_specs=pl.BlockSpec((1, 2 * BLK + heads, span), lambda i, g: (i, 0, 0)),
        ),
        compiler_params=LARGE,
    )(group.reshape(1), queries, out_grad, fwd_out, log_sum)


def finish_kernel(groups, me_ref, *refs):
    refs = list(refs)
    take = lambda n: [refs.pop(0) for _ in range(n)]
    parts, come, grads = take(groups), take(groups), take(groups)
    query_ref, key_ref, value_ref, held, key_s, value_s, in_sem, out_sem = refs
    span = held.shape[2]
    ins = [
        pltpu.make_async_copy(grads[mask], held.at[mask], in_sem.at[mask])
        for mask in range(groups)
    ]
    for copy in ins:
        copy.start()
    for mask in range(groups):
        at = pl.ds(pl.multiple_of((me_ref[0] ^ mask) * D_HEAD, D_HEAD), D_HEAD)
        total = parts[mask][...].astype(F32) + come[mask][...].astype(F32)
        key_s[:, at] = (total[:, 0:D_HEAD] * D_HEAD ** (-0.5)).astype(BF16)
        value_s[:, at] = total[:, D_HEAD : 2 * D_HEAD].astype(BF16)
    outs = [
        pltpu.make_async_copy(key_s, key_ref, out_sem.at[groups]),
        pltpu.make_async_copy(value_s, value_ref, out_sem.at[groups + 1]),
    ]
    for copy in outs:
        copy.start()
    for mask in range(groups):
        at = pl.ds(pl.multiple_of((me_ref[0] ^ mask) * span, span), span)
        ins[mask].wait()
        copy = pltpu.make_async_copy(held.at[mask], query_ref.at[:, at], out_sem.at[mask])
        copy.start()
        outs.append(copy)
    for copy in outs:
        copy.wait()


def finish(groups, me, parts, come, grads):
    tokens, span = grads[0].shape
    small = jax.ShapeDtypeStruct((tokens, groups * D_HEAD), BF16)
    return pl.pallas_call(
        functools.partial(finish_kernel, groups),
        out_shape=[jax.ShapeDtypeStruct((tokens, groups * span), BF16), small, small],
        in_specs=[SMEM] + [VMEM] * (2 * groups) + [ANY] * groups,
        out_specs=[HBM] * 3,
        scratch_shapes=[
            pltpu.VMEM((groups, tokens, span), BF16),
            pltpu.VMEM(small.shape, BF16),
            pltpu.VMEM(small.shape, BF16),
            pltpu.SemaphoreType.DMA((groups,)),
            pltpu.SemaphoreType.DMA((groups + 2,)),
        ],
        compiler_params=SMALL,
    )(me.reshape(1), *parts, *come, *grads)


def add_kernel(own_ref, come_ref, *outs):
    tokens = outs[0].shape[0]
    for at, out_ref in enumerate(outs):
        rows = pl.ds(at * tokens, tokens)
        out_ref[...] = (own_ref[rows, :] + come_ref[rows, :].astype(F32)).astype(BF16)


def add_sums(own, arrived, tokens):
    count = own.shape[0] // tokens
    return pl.pallas_call(
        add_kernel,
        out_shape=[jax.ShapeDtypeStruct((tokens, own.shape[1]), BF16)] * count,
        in_specs=[VMEM] * 2,
        out_specs=[VMEM] * count,
        compiler_params=SMALL,
    )(own, arrived)


def pair_kernel(chunks, places, ends, heads, factor, *refs):
    refs = list(refs)
    take = lambda n: [refs.pop(0) for _ in range(n)]
    count_ref, list_ref = take(2)
    pair_refs = take(chunks)
    (start_ref,) = take(1)
    kv_refs = take(places[-1][0] + 1)
    earlier = take(1)[0] if ends else None
    dq_refs = take(chunks)
    sum_refs = take(len(ends) if ends else 1)
    q_s, g_s, l_s, t_s, bias_s, p_s, s_s, dq_s, kv_s, pair_s, kv_sem, pair_sem = take(12)
    blocks = pair_refs[0].shape[0]
    tokens = blocks * BLK
    pair_copies = [
        pltpu.make_async_copy(pair_refs[c], pair_s.at[c], pair_sem.at[c]) for c in range(chunks)
    ]
    kv_copies = [
        pltpu.make_async_copy(
            kv_refs[ref].at[pl.ds(first, tokens)], kv_s.at[pl.ds(i * tokens, tokens)], kv_sem.at[i]
        )
        for i, (ref, first) in enumerate(places)
    ]
    for copy in pair_copies[:1] + kv_copies + pair_copies[1:]:
        copy.start()
    if ends:
        sum_ref, early_s, sem = take(3)
        early = pltpu.make_async_copy(earlier, early_s, sem)
        early.start()
    else:
        sum_ref = sum_refs[0]
    sum_ref[...] = jnp.zeros_like(sum_ref)
    for copy in kv_copies:
        copy.wait()
    wide = 2 * BLK
    for chunk in range(chunks):
        pair_copies[chunk].wait()

        def one_block(part, carry, chunk=chunk):
            row = chunk * blocks + part
            rows_at = pl.ds(2 * BLK, heads)
            pieces = pair_s[chunk, part, rows_at, 0 : 6 * BLK].astype(F32)
            pieces = [pieces[:, i * BLK : (i + 1) * BLK] for i in range(6)]
            log_rows = pieces[0] + pieces[1] + pieces[2]
            delta_rows = pieces[3] + pieces[4] + pieces[5]
            for head in range(heads):
                cols = pl.ds(head * D_HEAD, D_HEAD)
                out = pl.ds(head * BLK, BLK)
                q_s[out, :] = pair_s[chunk, part, 0:BLK, cols]
                g_s[out, :] = pair_s[chunk, part, BLK : 2 * BLK, cols]
                l_s[0:1, out] = log_rows[head : head + 1, :] * LOG2E
                t_s[0:1, out] = delta_rows[head : head + 1, :]
            dq_s[...] = jnp.zeros_like(dq_s)
            key_at = lax.broadcasted_iota(jnp.int32, (BLK, BLK), 0)
            query_at = lax.broadcasted_iota(jnp.int32, (BLK, BLK), 1)
            start_row = start_ref[pl.ds(row, 1), :]

            def one_pair(index, inner):
                code = list_ref[row * WINBLK + index]
                place = code // WINBLK
                distance = code % WINBLK
                keys_at = pl.ds(pl.multiple_of(place * BLK, BLK), BLK)
                key = kv_s[keys_at, 0:D_HEAD]
                value = kv_s[keys_at, D_HEAD : 2 * D_HEAD]
                there = key_at - distance * BLK
                allowed = (there <= query_at) & (there >= start_row)
                bias_s[...] = jnp.where(allowed, 0.0, LOWEST)
                for part_at in range(0, heads * BLK, wide):
                    span = pl.ds(part_at, wide)
                    score = lax.dot_general(key, q_s[span, :], NT, preferred_element_type=F32)
                    grad_w = lax.dot_general(value, g_s[span, :], NT, preferred_element_type=F32)
                    bias = bias_s[...]
                    bias = jnp.concatenate([bias, bias], axis=1)
                    weight = jnp.exp2(score * (factor * LOG2E) + (bias - l_s[0:1, span]))
                    p_s[:, span] = weight.astype(BF16)
                    s_s[:, span] = (weight * (grad_w - t_s[0:1, span])).astype(BF16)
                weights = p_s[...]
                grads = s_s[...]
                sum_ref[keys_at, D_HEAD : 2 * D_HEAD] += jnp.dot(
                    weights, g_s[...], preferred_element_type=F32
                )
                sum_ref[keys_at, 0:D_HEAD] += jnp.dot(
                    grads, q_s[...], preferred_element_type=F32
                )
                dq_s[...] += lax.dot_general(key, grads, TN, preferred_element_type=F32)
                return inner

            lax.fori_loop(0, count_ref[row], one_pair, 0)
            for head in range(heads):
                turned = jnp.transpose(dq_s[:, head * BLK : (head + 1) * BLK]) * factor
                dq_refs[chunk][
                    pl.ds(pl.multiple_of(part * BLK, BLK), BLK), pl.ds(head * D_HEAD, D_HEAD)
                ] = turned.astype(BF16)
            return carry

        lax.fori_loop(0, blocks, one_block, 0)
    if ends:
        early.wait()
        first = 0
        for out_ref in sum_refs:
            at = pl.ds(first, out_ref.shape[0])
            out_ref[...] = (sum_ref[at, :] + early_s[at, :]).astype(out_ref.dtype)
            first += out_ref.shape[0]


def run_pairs(heads, tokens, counts, lists, pairs, starts, kv, places, ends=(), earlier=None):
    chunks = len(pairs)
    factor = D_HEAD ** (-0.5)
    operands = [counts, lists, *pairs, starts, *kv]
    specs = [SMEM] * 2 + [HBM] * chunks + [VMEM] + [HBM] * len(kv)
    total = (len(places) * tokens, 2 * D_HEAD)
    scratch = [
        pltpu.VMEM((heads * BLK, D_HEAD), BF16),
        pltpu.VMEM((heads * BLK, D_HEAD), BF16),
        pltpu.VMEM((8, heads * BLK), F32),
        pltpu.VMEM((8, heads * BLK), F32),
        pltpu.VMEM((BLK, BLK), F32),
        pltpu.VMEM((BLK, heads * BLK), BF16),
        pltpu.VMEM((BLK, heads * BLK), BF16),
        pltpu.VMEM((D_HEAD, heads * BLK), F32),
        pltpu.VMEM(total, BF16),
        pltpu.VMEM((chunks,) + pairs[0].shape, BF16),
        pltpu.SemaphoreType.DMA((len(places),)),
        pltpu.SemaphoreType.DMA((chunks,)),
    ]
    outs = [jax.ShapeDtypeStruct((tokens, heads * D_HEAD), BF16)] * chunks
    if ends:
        operands.append(earlier)
        specs.append(HBM)
        outs += [jax.ShapeDtypeStruct((rows, total[1]), kind) for rows, kind in ends]
        scratch += [pltpu.VMEM(total, F32), pltpu.VMEM(total, F32), pltpu.SemaphoreType.DMA]
    else:
        outs.append(jax.ShapeDtypeStruct(total, F32))
    results = pl.pallas_call(
        functools.partial(pair_kernel, chunks, places, ends, heads, factor),
        out_shape=outs,
        in_specs=specs,
        out_specs=[VMEM] * len(outs),
        scratch_shapes=scratch,
        compiler_params=pltpu.CompilerParams(vmem_limit_bytes=24 << 20),
        cost_estimate=pl.CostEstimate(
            flops=10 * chunks * tokens * heads * D_HEAD * 6 * BLK,
            bytes_accessed=8 << 20,
            transcendentals=chunks * tokens * heads * 6 * BLK,
        ),
    )(*operands)
    return results[:chunks], results[chunks:]


def block_lists(flag_parts, seg_ids, me, plane, groups, blocks, back):
    plane_blocks = blocks * groups
    order = me ^ jnp.arange(groups, dtype=jnp.int32)
    row_at = (order[:, None] * blocks + jnp.arange(blocks, dtype=jnp.int32)).reshape(-1)
    flags = jnp.concatenate(flag_parts, axis=0)
    distance = jnp.arange(WINBLK, dtype=jnp.int32)
    query_block = plane * plane_blocks + row_at
    key_block = query_block[:, None] - distance[None, :]
    block_seg = seg_ids.reshape(-1, BLK)
    first_seg = block_seg[:, 0][query_block]
    last_seg = block_seg[:, BLK - 1][jnp.maximum(key_block, 0)]
    used = (flags > 0) & (key_block >= 0) & (last_seg >= first_seg[:, None])
    used = used.astype(jnp.int32)
    rank = jnp.sum(
        jnp.where(distance[None, None, :] < distance[None, :, None], used[:, None, :], 0), axis=2
    )
    rel = row_at[:, None] + back * plane_blocks - distance[None, :]
    in_plane = rel % plane_blocks
    place = (
        (rel // plane_blocks) * plane_blocks
        + ((in_plane // blocks) ^ me) * blocks
        + in_plane % blocks
    )
    code = place * WINBLK + distance[None, :]
    hit = (rank[:, None, :] == distance[None, :, None]) & (used[:, None, :] > 0)
    lists = jnp.sum(jnp.where(hit, code[:, None, :], 0), axis=2)
    counts = jnp.sum(used, axis=1)
    query_seg = block_seg[query_block]
    starts = (
        jnp.sum((seg_ids[:, None] < query_seg.reshape(-1)[None, :]).astype(jnp.int32), axis=0)
    ).reshape(-1, BLK) - query_block[:, None] * BLK
    return counts, lists, starts


def body(queries, keys, values, fwd_out, log_sum, out_grad, seg_ids, active):
    count = lax.axis_size("ctx")
    device = lax.axis_index("ctx")
    tokens = queries.shape[0]
    groups = keys.shape[1] // D_HEAD
    heads = queries.shape[1] // D_HEAD // groups
    blocks = tokens // BLK
    plane_blocks = blocks * groups
    back = WINBLK // plane_blocks
    me = device % groups
    plane = device // groups
    each = groups // HALVES

    def swap(value, mask):
        if mask == 0:
            return value
        return lax.ppermute(value, "ctx", [(s, s ^ mask) for s in range(count)])

    def shift(value, steps):
        moves = [(s, s + steps) for s in range(count) if 0 <= s + steps < count]
        return lax.ppermute(value, "ctx", moves)

    kv_send = pack_kv(groups, me, keys, values, active)
    kv_own = [swap(kv_send[mask], mask) for mask in range(groups)]
    pairs = []
    for mask in range(groups):
        sent = pack_pair(me ^ mask, heads, queries, out_grad, fwd_out, log_sum)
        pairs.append(swap(sent, mask))
    hops = [
        [
            jnp.concatenate([kv_own[h * each + i] for i in range(each)], axis=0)
            for h in range(HALVES)
        ]
    ]
    for _ in range(back):
        hops.append([shift(hops[-1][h], groups) for h in range(HALVES)])
    kv = [half for hop in hops[:0:-1] for half in hop] + kv_own
    places = [(i // each, (i % each) * (tokens + EXTRA)) for i in range(back * groups)]
    places += [(back * HALVES + m, 0) for m in range(groups)]

    counts, lists, starts = block_lists(
        [k[tokens : tokens + blocks, 0:WINBLK] for k in kv_own],
        seg_ids,
        me,
        plane,
        groups,
        blocks,
        back,
    )

    def members_run(members, ends, earlier):
        rows = slice(members[0] * blocks, (members[-1] + 1) * blocks)
        return run_pairs(
            heads,
            tokens,
            counts[rows],
            lists[rows].reshape(-1),
            [pairs[m] for m in members],
            starts[rows],
            kv,
            places,
            ends,
            earlier,
        )

    most = tuple(range(groups - 1))
    half = each * tokens
    ends = [(half, BF16)] * HALVES + [(half, F32)] * (back - 1) * HALVES
    ends += [(tokens, F32)] + [(tokens, BF16)] * (groups - 1)
    grads, sums = members_run(most, (), None)
    last, sums = members_run((groups - 1,), tuple(ends), sums[0])
    grads = list(grads) + list(last)

    parts = [swap(sums[back * HALVES + m], m) for m in range(groups)]
    come = [None] * groups
    for h in range(HALVES):
        sent = sums[h]
        for hop in range(1, back):
            arrived = shift(sent, -groups)
            sent = add_sums(sums[hop * HALVES + h], arrived, tokens)
        for i, m in enumerate(range(h * each, (h + 1) * each)):
            piece = sent[i] if back > 1 else sent[i * tokens : (i + 1) * tokens]
            moves = [(s, (s ^ m) - groups) for s in range(groups, count)]
            come[m] = lax.ppermute(piece, "ctx", moves)
    grads = [swap(grads[mask], mask) for mask in range(groups)]
    return tuple(finish(groups, me, parts, come, grads))


def solution(mesh):
    placed = (
        P("ctx", "kvh"),
        P("ctx", "kvh"),
        P("ctx", "kvh"),
        P("ctx", "kvh"),
        P("kvh", "ctx"),
        P("ctx", "kvh"),
        P(),
        P("ctx", None),
    )
    return jax.shard_map(
        body,
        mesh=mesh,
        in_specs=placed,
        out_specs=(P("ctx", "kvh"), P("ctx", "kvh"), P("ctx", "kvh")),
        check_vma=False,
    )
```

profile of v0, /device:TPU:14, one launch (start us, length us, event | category | flops | bytes accessed | tf_op | source)
XLA Modules:
  0.0 153.1 jit_solution(14786878007298367615)
XLA Ops:
  0.6 1.9 %shard_map.103 = (bf16[272,256]{1,0:T(8,128)(2,1)}, bf16[272,256]{1,0:T(8,128)(2,1)}, bf16[272,256]{1,0:T(8,128)(2,1)}, bf16[272,256]{1,0:T(8,128)(2,1)}) custom-call(s32[1]{0:T(128)} %bitcast.me_ref.group_ref, bf16[256,512]{1,0:T(8,128)(2,1)} %key_ref.1, bf16[256,512]{1,0:T(8,128)(2,1)} %value_ref.1, s32[2,16]{1,0:T(2,128)} %active_ref.1), custom_call_target="tpu_custom_call" | custom-call | tf_op jit(solution)/shard_map/pallas_call | solution.py:44
  3.1 1.5 collective-permute-start.2
  4.6 1.5 collective-permute-start
  6.1 2.5 %shard_map.106 = bf16[2,264,1024]{2,1,0:T(8,128)(2,1)} custom-call(s32[1]{0:T(128)} %bitcast.6.group_ref, bf16[256,4096]{1,0:T(8,128)(2,1)} %query_ref.7, bf16[256,4096]{1,0:T(8,128)(2,1)} %grad_ref.7, bf16[256,4096]{1,0:T(8,128)(2,1)} %fwd_ref.7, f32[32,256]{1,0:T(8,128)} %log_ref.7), custom_call_target="tpu_custom_call" | custom-call | tf_op jit(solution)/shard_map/pallas_call | solution.py:81
  9.0 2.4 %shard_map.107 = bf16[2,264,1024]{2,1,0:T(8,128)(2,1)} custom-call(s32[1]{0:T(128)} %bitcast.7.group_ref, bf16[256,4096]{1,0:T(8,128)(2,1)} %query_ref.7, bf16[256,4096]{1,0:T(8,128)(2,1)} %grad_ref.7, bf16[256,4096]{1,0:T(8,128)(2,1)} %fwd_ref.7, f32[32,256]{1,0:T(8,128)} %log_ref.7), custom_call_target="tpu_custom_call" | custom-call | tf_op jit(solution)/shard_map/pallas_call | solution.py:81
  14.6 2.8 %convert_reduce_fusion = s32[1024]{0:T(1024)S(1)} fusion(s32[1024]{0:T(1024)S(1)} %bitcast.20, s32[4096]{0:T(1024)} %param.14), kind=kLoop, calls=%fused_computation.3 | loop fusion | flops 12581888 | bytes 24576 | tf_op jit(solution)/shard_map/reduce_sum | solution.py:341
  18.1 1.6 %slice_reduce_fusion = (s32[32]{0:T(128)}, s32[32]{0:T(128)}) fusion(s32[32,128]{1,0:T(8,128)} %bitcast.18), kind=kLoop, calls=%fused_computation.10 | loop fusion | bytes 512 | tf_op jit(solution)/shard_map/slice | solution.py:321
  20.3 2.5 %shard_map.105.refs_2_ = bf16[2,264,1024]{2,1,0:T(8,128)(2,1)} custom-call(s32[1]{0:T(128)} %bitcast.me_ref.group_ref, bf16[256,4096]{1,0:T(8,128)(2,1)} %query_ref.7, bf16[256,4096]{1,0:T(8,128)(2,1)} %grad_ref.7, bf16[256,4096]{1,0:T(8,128)(2,1)} %fwd_ref.7, f32[32,256]{1,0:T(8,128)} %log_ref.7), custom_call_target="tpu_custom_call" | custom-call | tf_op jit(solution)/shard_map/pallas_call | solution.py:81
  30.0 2.5 %shard_map.104 = bf16[2,264,1024]{2,1,0:T(8,128)(2,1)} custom-call(s32[1]{0:T(128)} %bitcast.3.group_ref, bf16[256,4096]{1,0:T(8,128)(2,1)} %query_ref.7, bf16[256,4096]{1,0:T(8,128)(2,1)} %grad_ref.7, bf16[256,4096]{1,0:T(8,128)(2,1)} %fwd_ref.7, f32[32,256]{1,0:T(8,128)} %log_ref.7), custom_call_target="tpu_custom_call" | custom-call | tf_op jit(solution)/shard_map/pallas_call | solution.py:81
  32.5 2.4 %collective-permute-start.3 = (bf16[2,264,1024]{2,1,0:T(8,128)(2,1)}, bf16[2,264,1024]{2,1,0:T(8,128)(2,1)S(1)}, u32[]{:S(2)}, u32[]{:S(2)}) collective-permute-start(bf16[2,264,1024]{2,1,0:T(8,128)(2,1)} %shard_map.104), channel_id=1, source_target_pairs={{0,6},{2,4},{4,2},{6,0},{8,14},{10,12},{12,10},{14,8},{16,22},{18,... | collective-permute-start | bytes 3244040 | tf_op jit(solution)/shard_map/ppermute | solution.py:362
  35.9 3.5 %collective-permute-start.6 = (bf16[544,256]{1,0:T(8,128)(2,1)S(1)}, bf16[544,256]{1,0:T(8,128)(2,1)S(1)}, u32[]{:S(2)}, u32[]{:S(2)}) collective-permute-start(bf16[544,256]{1,0:T(8,128)(2,1)S(1)} %pad_maximum_fusion.1), channel_id=1, source_target_pairs={{0,8},{2,10},{4,12},{6,14},{8,16},{10,18},{12,20},{14,22},{16,24},... | collective-permute-start | bytes 835592 | tf_op jit(solution)/shard_map/ppermute | solution.py:366
  40.4 3.5 %collective-permute-start.4 = (bf16[544,256]{1,0:T(8,128)(2,1)S(1)}, bf16[544,256]{1,0:T(8,128)(2,1)S(1)}, u32[]{:S(2)}, u32[]{:S(2)}) collective-permute-start(bf16[544,256]{1,0:T(8,128)(2,1)S(1)} %pad_maximum_fusion), channel_id=1, source_target_pairs={{0,8},{2,10},{4,12},{6,14},{8,16},{10,18},{12,20},{14,22},{16,24},... | collective-permute-start | bytes 835592 | tf_op jit(solution)/shard_map/ppermute | solution.py:366
  46.7 3.2 %collective-permute-start.7 = (bf16[544,256]{1,0:T(8,128)(2,1)S(1)}, bf16[544,256]{1,0:T(8,128)(2,1)S(1)}, u32[]{:S(2)}, u32[]{:S(2)}) collective-permute-start(bf16[544,256]{1,0:T(8,128)(2,1)S(1)} %collective-permute-done.6.refs_9_.refs_7_), channel_id=1, source_target_pairs={{0,8},{2,10},{4,12},{6,14},{8,16},{10,18},{12,20},{14,22},{16,24},... | collective-permute-start | bytes 835592 | tf_op jit(solution)/shard_map/ppermute | solution.py:366
  49.9 2.3 %collective-permute-done.4.refs_8_.refs_6_ = bf16[544,256]{1,0:T(8,128)(2,1)S(1)} collective-permute-done((bf16[544,256]{1,0:T(8,128)(2,1)S(1)}, bf16[544,256]{1,0:T(8,128)(2,1)S(1)}, u32[]{:S(2)}, u32[]{:S(2)}) %collective-permute-start.4) | collective-permute-done | bytes 278560 | tf_op jit(solution)/shard_map/ppermute | solution.py:366
  52.3 3.6 %collective-permute-start.5 = (bf16[544,256]{1,0:T(8,128)(2,1)S(1)}, bf16[544,256]{1,0:T(8,128)(2,1)S(1)}, u32[]{:S(2)}, u32[]{:S(2)}) collective-permute-start(bf16[544,256]{1,0:T(8,128)(2,1)S(1)} %collective-permute-done.4.refs_8_.refs_6_), channel_id=1, source_target_pairs={{0,8},{2,10},{4,12},{6,14},{8,16},{10,18},{12,20},{14,22},{16,24},... | collective-permute-start | bytes 835592 | tf_op jit(solution)/shard_map/ppermute | solution.py:366
  58.2 4.2 %collective-permute-done.5.refs_6_.refs_4_ = bf16[544,256]{1,0:T(8,128)(2,1)S(1)} collective-permute-done((bf16[544,256]{1,0:T(8,128)(2,1)S(1)}, bf16[544,256]{1,0:T(8,128)(2,1)S(1)}, u32[]{:S(2)}, u32[]{:S(2)}) %collective-permute-start.5) | collective-permute-done | bytes 278560 | tf_op jit(solution)/shard_map/ppermute | solution.py:366
  65.3 20.9 %shard_map.108 = (bf16[256,1024]{1,0:T(8,128)(2,1)S(1)}, bf16[256,1024]{1,0:T(8,128)(2,1)S(1)}, bf16[256,1024]{1,0:T(8,128)(2,1)S(1)}, f32[3072,256]{1,0:T(8,128)S(1)}) custom-call(s32[6]{0:T(128)S(1)} %bitcast.16, s32[96]{0:T(128)S(1)} %reshape.347.refs_1_, bf16[2,264,1024]{2,1,0:T(8,128)(2,1)S(1)} %copy-done, ...), custom_call_target="tpu_custom_call" | custom-call | flops 6039797760 | bytes 8388608 | tf_op jit(solution)/shard_map/pallas_call | solution.py:296
  86.2 9.5 %shard_map.109 = (bf16[256,1024]{1,0:T(8,128)(2,1)S(1)}, bf16[512,256]{1,0:T(8,128)(2,1)S(1)}, bf16[512,256]{1,0:T(8,128)(2,1)S(1)}, f32[512,256]{1,0:T(8,128)S(...) custom-call(s32[2]{0:T(128)S(1)} %slice.42.refs_0_, ...), custom_call_target="tpu_custom_call" | custom-call | flops 2013265920 | bytes 8388608 | tf_op jit(solution)/shard_map/pallas_call | solution.py:296
  95.7 1.9 %collective-permute-start.16 = (bf16[512,256]{1,0:T(8,128)(2,1)S(1)}, bf16[512,256]{1,0:T(8,128)(2,1)S(1)}, u32[]{:S(2)}, u32[]{:S(2)}) collective-permute-start(bf16[512,256]{1,0:T(8,128)(2,1)S(1)} %get-tuple-element.38), channel_id=1, source_target_pairs={{8,0},{10,2},{12,4},{14,6},{16,8},{18,10},{20,12},{22,14},{24,16},... | collective-permute-start | bytes 786440 | tf_op jit(solution)/shard_map/ppermute | solution.py:366
  98.8 1.9 %collective-permute-start.13 = (bf16[512,256]{1,0:T(8,128)(2,1)S(1)}, bf16[512,256]{1,0:T(8,128)(2,1)S(1)}, u32[]{:S(2)}, u32[]{:S(2)}) collective-permute-start(bf16[512,256]{1,0:T(8,128)(2,1)S(1)} %get-tuple-element.34), channel_id=1, source_target_pairs={{8,0},{10,2},{12,4},{14,6},{16,8},{18,10},{20,12},{22,14},{24,16},... | collective-permute-start | bytes 786440 | tf_op jit(solution)/shard_map/ppermute | solution.py:366
  100.7 2.5 %collective-permute-start.21 = (bf16[256,1024]{1,0:T(8,128)(2,1)S(1)}, bf16[256,1024]{1,0:T(8,128)(2,1)S(1)}, u32[]{:S(2)}, u32[]{:S(2)}) collective-permute-start(bf16[256,1024]{1,0:T(8,128)(2,1)S(1)} %get-tuple-element.44), channel_id=1, source_target_pairs={{0,6},{2,4},{4,2},{6,0},{8,14},{10,12},{12,10},{14,8},{16,22},{18,... | collective-permute-start | bytes 1572872 | tf_op jit(solution)/shard_map/ppermute | solution.py:362
  103.7 9.8 %collective-permute-done.11.refs_2_ = bf16[256,256]{1,0:T(8,128)(2,1)S(1)} collective-permute-done((bf16[256,256]{1,0:T(8,128)(2,1)S(1)}, bf16[256,256]{1,0:T(8,128)(2,1)S(1)}, u32[]{:S(2)}, u32[]{:S(2)}) %collective-permute-start.11) | collective-permute-done | bytes 131104 | tf_op jit(solution)/shard_map/ppermute | solution.py:362
  113.5 4.1 %collective-permute-start.12 = (bf16[256,256]{1,0:T(8,128)(2,1)S(1)}, bf16[256,256]{1,0:T(8,128)(2,1)S(1)}, u32[]{:S(2)}, u32[]{:S(2)}) collective-permute-start(bf16[256,256]{1,0:T(8,128)(2,1)S(1)} %get-tuple-element.32), channel_id=1, source_target_pairs={{0,6},{2,4},{4,2},{6,0},{8,14},{10,12},{12,10},{14,8},{16,22},{18,... | collective-permute-start | bytes 393224 | tf_op jit(solution)/shard_map/ppermute | solution.py:362
  117.6 10.4 %collective-permute-done.12.refs_3_ = bf16[256,256]{1,0:T(8,128)(2,1)S(1)} collective-permute-done((bf16[256,256]{1,0:T(8,128)(2,1)S(1)}, bf16[256,256]{1,0:T(8,128)(2,1)S(1)}, u32[]{:S(2)}, u32[]{:S(2)}) %collective-permute-start.12) | collective-permute-done | bytes 131104 | tf_op jit(solution)/shard_map/ppermute | solution.py:362
  128.1 1.9 %collective-permute-start.17 = (bf16[256,256]{1,0:T(8,128)(2,1)S(1)}, bf16[256,256]{1,0:T(8,128)(2,1)S(1)}, u32[]{:S(2)}, u32[]{:S(2)}) collective-permute-start(bf16[256,256]{1,0:T(8,128)(2,1)S(1)} %get-tuple-element.39), channel_id=1, source_target_pairs={{8,4},{10,6},{12,0},{14,2},{16,12},{18,14},{20,8},{22,10},{24,20},... | collective-permute-start | bytes 393224 | tf_op jit(solution)/shard_map/ppermute | solution.py:429
  130.0 1.9 %collective-permute-start.18 = (bf16[256,256]{1,0:T(8,128)(2,1)S(1)}, bf16[256,256]{1,0:T(8,128)(2,1)S(1)}, u32[]{:S(2)}, u32[]{:S(2)}) collective-permute-start(bf16[256,256]{1,0:T(8,128)(2,1)S(1)} %get-tuple-element.40), channel_id=1, source_target_pairs={{8,6},{10,4},{12,2},{14,0},{16,14},{18,12},{20,10},{22,8},{24,22},... | collective-permute-start | bytes 393224 | tf_op jit(solution)/shard_map/ppermute | solution.py:429
  132.0 4.3 %collective-permute-done.17.refs_6_ = bf16[256,256]{1,0:T(8,128)(2,1)S(1)} collective-permute-done((bf16[256,256]{1,0:T(8,128)(2,1)S(1)}, bf16[256,256]{1,0:T(8,128)(2,1)S(1)}, u32[]{:S(2)}, u32[]{:S(2)}) %collective-permute-start.17) | collective-permute-done | bytes 131104 | tf_op jit(solution)/shard_map/ppermute | solution.py:429
  136.3 1.9 %collective-permute-start.14 = (bf16[256,256]{1,0:T(8,128)(2,1)S(1)}, bf16[256,256]{1,0:T(8,128)(2,1)S(1)}, u32[]{:S(2)}, u32[]{:S(2)}) collective-permute-start(bf16[256,256]{1,0:T(8,128)(2,1)S(1)} %get-tuple-element.35), channel_id=1, source_target_pairs={{8,0},{10,2},{12,4},{14,6},{16,8},{18,10},{20,12},{22,14},{24,16},... | collective-permute-start | bytes 393224 | tf_op jit(solution)/shard_map/ppermute | solution.py:429
  138.7 2.0 %collective-permute-start.15 = (bf16[256,256]{1,0:T(8,128)(2,1)S(1)}, bf16[256,256]{1,0:T(8,128)(2,1)S(1)}, u32[]{:S(2)}, u32[]{:S(2)}) collective-permute-start(bf16[256,256]{1,0:T(8,128)(2,1)S(1)} %get-tuple-element.36), channel_id=1, source_target_pairs={{8,2},{10,0},{12,6},{14,4},{16,10},{18,8},{20,14},{22,12},{24,18},... | collective-permute-start | bytes 393224 | tf_op jit(solution)/shard_map/ppermute | solution.py:429
  140.7 7.5 %collective-permute-done.14.refs_4_ = bf16[256,256]{1,0:T(8,128)(2,1)S(1)} collective-permute-done((bf16[256,256]{1,0:T(8,128)(2,1)S(1)}, bf16[256,256]{1,0:T(8,128)(2,1)S(1)}, u32[]{:S(2)}, u32[]{:S(2)}) %collective-permute-start.14) | collective-permute-done | bytes 131104 | tf_op jit(solution)/shard_map/ppermute | solution.py:429
  148.2 3.0 %collective-permute-done.15.refs_5_ = bf16[256,256]{1,0:T(8,128)(2,1)S(1)} collective-permute-done((bf16[256,256]{1,0:T(8,128)(2,1)S(1)}, bf16[256,256]{1,0:T(8,128)(2,1)S(1)}, u32[]{:S(2)}, u32[]{:S(2)}) %collective-permute-start.15) | collective-permute-done | bytes 131104 | tf_op jit(solution)/shard_map/ppermute | solution.py:429
  151.2 1.8 %shard_map.112 = (bf16[256,4096]{1,0:T(8,128)(2,1)}, bf16[256,512]{1,0:T(8,128)(2,1)}, bf16[256,512]{1,0:T(8,128)(2,1)}) custom-call(s32[1]{0:T(128)} %bitcast.me_ref.group_ref, f32[256,256]{1,0:T(8,128)S(1)} %get-tuple-element.29.refs_0_, bf16[256,256]{1,0:T(8,128)(2,1)S(1)} %collective-permute-done.10.refs_1_, ...), custom_call_target="tpu_custom_call" | custom-call | tf_op jit(solution)/shard_map/pallas_call | solution.py:130
  (75 shorter events, 24.7 us)
Async XLA Ops:
  2.6 29.9 %collective-permute-start.1 = (bf16[272,256]{1,0:T(8,128)(2,1)}, bf16[272,256]{1,0:T(8,128)(2,1)}, u32[]{:S(2)}, u32[]{:S(2)}) collective-permute-start(bf16[272,256]{1,0:T(8,128)(2,1)} %get-tuple-element.26), channel_id=1, source_target_pairs={{0,4},{2,6},{4,0},{6,2},{8,12},{10,14},{12,8},{14,10},{16,20},{18,... | collective-permute-start | bytes 417800 | tf_op jit(solution)/shard_map/ppermute | solution.py:362
  3.1 31.9 %collective-permute-start.2 = (bf16[272,256]{1,0:T(8,128)(2,1)}, bf16[272,256]{1,0:T(8,128)(2,1)}, u32[]{:S(2)}, u32[]{:S(2)}) collective-permute-start(bf16[272,256]{1,0:T(8,128)(2,1)} %get-tuple-element.27), channel_id=1, source_target_pairs={{0,6},{2,4},{4,2},{6,0},{8,14},{10,12},{12,10},{14,8},{16,22},{18,... | collective-permute-start | bytes 417800 | tf_op jit(solution)/shard_map/ppermute | solution.py:362
  4.6 34.9 %collective-permute-start = (bf16[272,256]{1,0:T(8,128)(2,1)}, bf16[272,256]{1,0:T(8,128)(2,1)}, u32[]{:S(2)}, u32[]{:S(2)}) collective-permute-start(bf16[272,256]{1,0:T(8,128)(2,1)} %get-tuple-element.25), channel_id=1, source_target_pairs={{0,2},{2,0},{4,6},{6,4},{8,10},{10,8},{12,14},{14,12},{16,18},{18,... | collective-permute-start | bytes 417800 | tf_op jit(solution)/shard_map/ppermute | solution.py:362
  8.5 53.9 %collective-permute-start.8 = (bf16[2,264,1024]{2,1,0:T(8,128)(2,1)}, bf16[2,264,1024]{2,1,0:T(8,128)(2,1)}, u32[]{:S(2)}, u32[]{:S(2)}) collective-permute-start(bf16[2,264,1024]{2,1,0:T(8,128)(2,1)} %shard_map.106), channel_id=1, source_target_pairs={{0,2},{2,0},{4,6},{6,4},{8,10},{10,8},{12,14},{14,12},{16,18},{18,... | collective-permute-start | bytes 3244040 | tf_op jit(solution)/shard_map/ppermute | solution.py:362
  11.5 51.0 %collective-permute-start.9 = (bf16[2,264,1024]{2,1,0:T(8,128)(2,1)}, bf16[2,264,1024]{2,1,0:T(8,128)(2,1)}, u32[]{:S(2)}, u32[]{:S(2)}) collective-permute-start(bf16[2,264,1024]{2,1,0:T(8,128)(2,1)} %shard_map.107), channel_id=1, source_target_pairs={{0,4},{2,6},{4,0},{6,2},{8,12},{10,14},{12,8},{14,10},{16,20},{18,... | collective-permute-start | bytes 3244040 | tf_op jit(solution)/shard_map/ppermute | solution.py:362
  12.7 0.5 copy-start.8
  13.3 6.5 %copy-start.7 = (s32[1024]{0:T(1024)}, s32[1024]{0:T(1024)S(1)}, u32[]{:S(2)}) copy-start(s32[1024]{0:T(1024)S(1)} %pad_clamp_fusion) | copy-start | bytes 12292
  22.8 0.7 copy-start.4
  23.5 2.2 %copy-start.5 = (s32[32]{0:T(128)S(1)}, s32[32]{0:T(128)}, u32[]{:S(2)}) copy-start(s32[32]{0:T(128)} %get-tuple-element.45) | copy-start | bytes 388
  23.5 4.7 %copy-start.6 = (s32[4,2]{1,0:T(4,128)S(1)}, s32[4,2]{1,0:T(4,128)}, u32[]{:S(2)}) copy-start(s32[4,2]{1,0:T(4,128)} %get-tuple-element.49) | copy-start | bytes 100
  32.5 53.7 %collective-permute-start.3 = (bf16[2,264,1024]{2,1,0:T(8,128)(2,1)}, bf16[2,264,1024]{2,1,0:T(8,128)(2,1)S(1)}, u32[]{:S(2)}, u32[]{:S(2)}) collective-permute-start(bf16[2,264,1024]{2,1,0:T(8,128)(2,1)} %shard_map.104), channel_id=1, source_target_pairs={{0,6},{2,4},{4,2},{6,0},{8,14},{10,12},{12,10},{14,8},{16,22},{18,... | collective-permute-start | bytes 3244040 | tf_op jit(solution)/shard_map/ppermute | solution.py:362
  35.9 10.7 %collective-permute-start.6 = (bf16[544,256]{1,0:T(8,128)(2,1)S(1)}, bf16[544,256]{1,0:T(8,128)(2,1)S(1)}, u32[]{:S(2)}, u32[]{:S(2)}) collective-permute-start(bf16[544,256]{1,0:T(8,128)(2,1)S(1)} %pad_maximum_fusion.1), channel_id=1, source_target_pairs={{0,8},{2,10},{4,12},{6,14},{8,16},{10,18},{12,20},{14,22},{16,24},... | collective-permute-start | bytes 835592 | tf_op jit(solution)/shard_map/ppermute | solution.py:366
  40.4 11.8 %collective-permute-start.4 = (bf16[544,256]{1,0:T(8,128)(2,1)S(1)}, bf16[544,256]{1,0:T(8,128)(2,1)S(1)}, u32[]{:S(2)}, u32[]{:S(2)}) collective-permute-start(bf16[544,256]{1,0:T(8,128)(2,1)S(1)} %pad_maximum_fusion), channel_id=1, source_target_pairs={{0,8},{2,10},{4,12},{6,14},{8,16},{10,18},{12,20},{14,22},{16,24},... | collective-permute-start | bytes 835592 | tf_op jit(solution)/shard_map/ppermute | solution.py:366
  46.7 11.5 %collective-permute-start.7 = (bf16[544,256]{1,0:T(8,128)(2,1)S(1)}, bf16[544,256]{1,0:T(8,128)(2,1)S(1)}, u32[]{:S(2)}, u32[]{:S(2)}) collective-permute-start(bf16[544,256]{1,0:T(8,128)(2,1)S(1)} %collective-permute-done.6.refs_9_.refs_7_), channel_id=1, source_target_pairs={{0,8},{2,10},{4,12},{6,14},{8,16},{10,18},{12,20},{14,22},{16,24},... | collective-permute-start | bytes 835592 | tf_op jit(solution)/shard_map/ppermute | solution.py:366
  52.3 10.2 %collective-permute-start.5 = (bf16[544,256]{1,0:T(8,128)(2,1)S(1)}, bf16[544,256]{1,0:T(8,128)(2,1)S(1)}, u32[]{:S(2)}, u32[]{:S(2)}) collective-permute-start(bf16[544,256]{1,0:T(8,128)(2,1)S(1)} %collective-permute-done.4.refs_8_.refs_6_), channel_id=1, source_target_pairs={{0,8},{2,10},{4,12},{6,14},{8,16},{10,18},{12,20},{14,22},{16,24},... | collective-permute-start | bytes 835592 | tf_op jit(solution)/shard_map/ppermute | solution.py:366
  62.5 1.2 copy-start
  63.7 0.9 copy-start.1
  64.6 0.7 copy-start.2
  65.3 20.9 %copy-start.3 = (s32[2,128]{1,0:T(2,128)S(1)}, s32[2,128]{1,0:T(2,128)}, u32[]{:S(2)}) copy-start(s32[2,128]{1,0:T(2,128)} %slice.44.refs_3_) | copy-start | bytes 3076
  95.7 17.8 %collective-permute-start.16 = (bf16[512,256]{1,0:T(8,128)(2,1)S(1)}, bf16[512,256]{1,0:T(8,128)(2,1)S(1)}, u32[]{:S(2)}, u32[]{:S(2)}) collective-permute-start(bf16[512,256]{1,0:T(8,128)(2,1)S(1)} %get-tuple-element.38), channel_id=1, source_target_pairs={{8,0},{10,2},{12,4},{14,6},{16,8},{18,10},{20,12},{22,14},{24,16},... | collective-permute-start | bytes 786440 | tf_op jit(solution)/shard_map/ppermute | solution.py:366
  97.7 5.6 %collective-permute-start.10 = (bf16[256,256]{1,0:T(8,128)(2,1)S(1)}, bf16[256,256]{1,0:T(8,128)(2,1)S(1)}, u32[]{:S(2)}, u32[]{:S(2)}) collective-permute-start(bf16[256,256]{1,0:T(8,128)(2,1)S(1)} %get-tuple-element.30), channel_id=1, source_target_pairs={{0,2},{2,0},{4,6},{6,4},{8,10},{10,8},{12,14},{14,12},{16,18},{18,... | collective-permute-start | bytes 393224 | tf_op jit(solution)/shard_map/ppermute | solution.py:362
  98.3 15.2 %collective-permute-start.11 = (bf16[256,256]{1,0:T(8,128)(2,1)S(1)}, bf16[256,256]{1,0:T(8,128)(2,1)S(1)}, u32[]{:S(2)}, u32[]{:S(2)}) collective-permute-start(bf16[256,256]{1,0:T(8,128)(2,1)S(1)} %get-tuple-element.31), channel_id=1, source_target_pairs={{0,4},{2,6},{4,0},{6,2},{8,12},{10,14},{12,8},{14,10},{16,20},{18,... | collective-permute-start | bytes 393224 | tf_op jit(solution)/shard_map/ppermute | solution.py:362
  98.8 31.2 %collective-permute-start.13 = (bf16[512,256]{1,0:T(8,128)(2,1)S(1)}, bf16[512,256]{1,0:T(8,128)(2,1)S(1)}, u32[]{:S(2)}, u32[]{:S(2)}) collective-permute-start(bf16[512,256]{1,0:T(8,128)(2,1)S(1)} %get-tuple-element.34), channel_id=1, source_target_pairs={{8,0},{10,2},{12,4},{14,6},{16,8},{18,10},{20,12},{22,14},{24,16},... | collective-permute-start | bytes 786440 | tf_op jit(solution)/shard_map/ppermute | solution.py:366
  100.7 50.5 %collective-permute-start.21 = (bf16[256,1024]{1,0:T(8,128)(2,1)S(1)}, bf16[256,1024]{1,0:T(8,128)(2,1)S(1)}, u32[]{:S(2)}, u32[]{:S(2)}) collective-permute-start(bf16[256,1024]{1,0:T(8,128)(2,1)S(1)} %get-tuple-element.44), channel_id=1, source_target_pairs={{0,6},{2,4},{4,2},{6,0},{8,14},{10,12},{12,10},{14,8},{16,22},{18,... | collective-permute-start | bytes 1572872 | tf_op jit(solution)/shard_map/ppermute | solution.py:362
  103.3 48.0 %collective-permute-start.19 = (bf16[256,1024]{1,0:T(8,128)(2,1)S(1)}, bf16[256,1024]{1,0:T(8,128)(2,1)S(1)}, u32[]{:S(2)}, u32[]{:S(2)}) collective-permute-start(bf16[256,1024]{1,0:T(8,128)(2,1)S(1)} %get-tuple-element.42), channel_id=1, source_target_pairs={{0,2},{2,0},{4,6},{6,4},{8,10},{10,8},{12,14},{14,12},{16,18},{18,... | collective-permute-start | bytes 1572872 | tf_op jit(solution)/shard_map/ppermute | solution.py:362
  113.5 37.7 %collective-permute-start.20 = (bf16[256,1024]{1,0:T(8,128)(2,1)S(1)}, bf16[256,1024]{1,0:T(8,128)(2,1)S(1)}, u32[]{:S(2)}, u32[]{:S(2)}) collective-permute-start(bf16[256,1024]{1,0:T(8,128)(2,1)S(1)} %get-tuple-element.43), channel_id=1, source_target_pairs={{0,4},{2,6},{4,0},{6,2},{8,12},{10,14},{12,8},{14,10},{16,20},{18,... | collective-permute-start | bytes 1572872 | tf_op jit(solution)/shard_map/ppermute | solution.py:362
  113.5 14.6 %collective-permute-start.12 = (bf16[256,256]{1,0:T(8,128)(2,1)S(1)}, bf16[256,256]{1,0:T(8,128)(2,1)S(1)}, u32[]{:S(2)}, u32[]{:S(2)}) collective-permute-start(bf16[256,256]{1,0:T(8,128)(2,1)S(1)} %get-tuple-element.32), channel_id=1, source_target_pairs={{0,6},{2,4},{4,2},{6,0},{8,14},{10,12},{12,10},{14,8},{16,22},{18,... | collective-permute-start | bytes 393224 | tf_op jit(solution)/shard_map/ppermute | solution.py:362
  128.1 8.2 %collective-permute-start.17 = (bf16[256,256]{1,0:T(8,128)(2,1)S(1)}, bf16[256,256]{1,0:T(8,128)(2,1)S(1)}, u32[]{:S(2)}, u32[]{:S(2)}) collective-permute-start(bf16[256,256]{1,0:T(8,128)(2,1)S(1)} %get-tuple-element.39), channel_id=1, source_target_pairs={{8,4},{10,6},{12,0},{14,2},{16,12},{18,14},{20,8},{22,10},{24,20},... | collective-permute-start | bytes 393224 | tf_op jit(solution)/shard_map/ppermute | solution.py:429
  130.0 8.7 %collective-permute-start.18 = (bf16[256,256]{1,0:T(8,128)(2,1)S(1)}, bf16[256,256]{1,0:T(8,128)(2,1)S(1)}, u32[]{:S(2)}, u32[]{:S(2)}) collective-permute-start(bf16[256,256]{1,0:T(8,128)(2,1)S(1)} %get-tuple-element.40), channel_id=1, source_target_pairs={{8,6},{10,4},{12,2},{14,0},{16,14},{18,12},{20,10},{22,8},{24,22},... | collective-permute-start | bytes 393224 | tf_op jit(solution)/shard_map/ppermute | solution.py:429
  136.3 11.9 %collective-permute-start.14 = (bf16[256,256]{1,0:T(8,128)(2,1)S(1)}, bf16[256,256]{1,0:T(8,128)(2,1)S(1)}, u32[]{:S(2)}, u32[]{:S(2)}) collective-permute-start(bf16[256,256]{1,0:T(8,128)(2,1)S(1)} %get-tuple-element.35), channel_id=1, source_target_pairs={{8,0},{10,2},{12,4},{14,6},{16,8},{18,10},{20,12},{22,14},{24,16},... | collective-permute-start | bytes 393224 | tf_op jit(solution)/shard_map/ppermute | solution.py:429
  138.7 12.6 %collective-permute-start.15 = (bf16[256,256]{1,0:T(8,128)(2,1)S(1)}, bf16[256,256]{1,0:T(8,128)(2,1)S(1)}, u32[]{:S(2)}, u32[]{:S(2)}) collective-permute-start(bf16[256,256]{1,0:T(8,128)(2,1)S(1)} %get-tuple-element.36), channel_id=1, source_target_pairs={{8,2},{10,0},{12,6},{14,4},{16,10},{18,8},{20,14},{22,12},{24,18},... | collective-permute-start | bytes 393224 | tf_op jit(solution)/shard_map/ppermute | solution.py:429
where the time goes:
time: 156 us; the launch traced here: 153 us
  Pallas kernels  44.1 us (28%)
  waiting for transfers between devices  42.9 us (28%)
  starting transfers between devices  40.6 us (26%)
  local copies, waits for them, and re-layouts  15.7 us (10%)
  other arithmetic  8.86 us (6%)
    pallas_call x2, Pallas kernels, run_pairs(): pl.pallas_call(functools.partial(pair_kernel, chunks, places, ends, heads...  30.4 us
    ppermute x12, waiting for transfers between devices, swap(): return lax.ppermute(value, 'ctx', [(s, s ^ mask) for s in range(count)])  20.3 us
    ppermute x6, starting transfers between devices, shift(): return lax.ppermute(value, 'ctx', moves)  17.7 us
    ppermute x4, waiting for transfers between devices, body(): come[m] = lax.ppermute(piece, 'ctx', moves)  15.3 us
    ppermute x12, starting transfers between devices, swap(): return lax.ppermute(value, 'ctx', [(s, s ^ mask) for s in range(count)])  15.1 us
    pallas_call x4, Pallas kernels, pack_pair(): pl.pallas_call(functools.partial(pair_pack_kernel, heads), out_shape=jax....  9.83 us
    ppermute x4, starting transfers between devices, body(): come[m] = lax.ppermute(piece, 'ctx', moves)  7.75 us
    ppermute x6, waiting for transfers between devices, shift(): return lax.ppermute(value, 'ctx', moves)  7.32 us
  transfers between devices with their start and end apart: 22, of which 10 were waited for; matrix products, arithmetic and copies ran while one was open for 14% of the time, Pallas kernels for 20%

commit v1 on v0

--- a/solution.py
+++ b/solution.py
@@ -186,12 +186,13 @@
     for copy in pair_copies[:1] + kv_copies + pair_copies[1:]:
         copy.start()
     if ends:
-        sum_ref, early_s, sem = take(3)
-        early = pltpu.make_async_copy(earlier, early_s, sem)
+        sum_ref, sem = take(2)
+        early = pltpu.make_async_copy(earlier, sum_ref, sem)
         early.start()
+        early.wait()
     else:
         sum_ref = sum_refs[0]
-    sum_ref[...] = jnp.zeros_like(sum_ref)
+        sum_ref[...] = jnp.zeros_like(sum_ref)
     for copy in kv_copies:
         copy.wait()
     wide = 2 * BLK
@@ -217,16 +218,22 @@
             query_at = lax.broadcasted_iota(jnp.int32, (BLK, BLK), 1)
             start_row = start_ref[pl.ds(row, 1), :]
 
-            def one_pair(index, inner):
-                code = list_ref[row * WINBLK + index]
-                place = code // WINBLK
-                distance = code % WINBLK
-                keys_at = pl.ds(pl.multiple_of(place * BLK, BLK), BLK)
-                key = kv_s[keys_at, 0:D_HEAD]
-                value = kv_s[keys_at, D_HEAD : 2 * D_HEAD]
+            def key_place(index):
+                code = list_ref[row * WINBLK + jnp.minimum(index, WINBLK - 1)]
+                distance = jnp.where(index < count_ref[row], code % WINBLK, -2)
                 there = key_at - distance * BLK
                 allowed = (there <= query_at) & (there >= start_row)
-                bias_s[...] = jnp.where(allowed, 0.0, LOWEST)
+                place = pl.ds(pl.multiple_of(code // WINBLK * BLK, BLK), BLK)
+                return place, jnp.where(allowed, 0.0, LOWEST)
+
+            def two_blocks(index, inner):
+                first, first_bias = key_place(2 * index)
+                second, second_bias = key_place(2 * index + 1)
+                bias_s[0:BLK, :] = first_bias
+                bias_s[BLK : 2 * BLK, :] = second_bias
+                key = jnp.concatenate([kv_s[first, 0:D_HEAD], kv_s[second, 0:D_HEAD]], axis=0)
+                both = pl.ds(D_HEAD, D_HEAD)
+                value = jnp.concatenate([kv_s[first, both], kv_s[second, both]], axis=0)
                 for part_at in range(0, heads * BLK, wide):
                     span = pl.ds(part_at, wide)
                     score = lax.dot_general(key, q_s[span, :], NT, preferred_element_type=F32)
@@ -236,18 +243,17 @@
                     weight = jnp.exp2(score * (factor * LOG2E) + (bias - l_s[0:1, span]))
                     p_s[:, span] = weight.astype(BF16)
                     s_s[:, span] = (weight * (grad_w - t_s[0:1, span])).astype(BF16)
-                weights = p_s[...]
                 grads = s_s[...]
-                sum_ref[keys_at, D_HEAD : 2 * D_HEAD] += jnp.dot(
-                    weights, g_s[...], preferred_element_type=F32
-                )
-                sum_ref[keys_at, 0:D_HEAD] += jnp.dot(
-                    grads, q_s[...], preferred_element_type=F32
-                )
+                value_sum = jnp.dot(p_s[...], g_s[...], preferred_element_type=F32)
+                key_sum = jnp.dot(grads, q_s[...], preferred_element_type=F32)
+                sum_ref[first, D_HEAD : 2 * D_HEAD] += value_sum[0:BLK]
+                sum_ref[first, 0:D_HEAD] += key_sum[0:BLK]
+                sum_ref[second, D_HEAD : 2 * D_HEAD] += value_sum[BLK : 2 * BLK]
+                sum_ref[second, 0:D_HEAD] += key_sum[BLK : 2 * BLK]
                 dq_s[...] += lax.dot_general(key, grads, TN, preferred_element_type=F32)
                 return inner
 
-            lax.fori_loop(0, count_ref[row], one_pair, 0)
+            lax.fori_loop(0, (count_ref[row] + 1) // 2, two_blocks, 0)
             for head in range(heads):
                 turned = jnp.transpose(dq_s[:, head * BLK : (head + 1) * BLK]) * factor
                 dq_refs[chunk][
@@ -257,11 +263,10 @@
 
         lax.fori_loop(0, blocks, one_block, 0)
     if ends:
-        early.wait()
         first = 0
         for out_ref in sum_refs:
             at = pl.ds(first, out_ref.shape[0])
-            out_ref[...] = (sum_ref[at, :] + early_s[at, :]).astype(out_ref.dtype)
+            out_ref[...] = sum_ref[at, :].astype(out_ref.dtype)
             first += out_ref.shape[0]
 
 
@@ -276,9 +281,9 @@
         pltpu.VMEM((heads * BLK, D_HEAD), BF16),
         pltpu.VMEM((8, heads * BLK), F32),
         pltpu.VMEM((8, heads * BLK), F32),
-        pltpu.VMEM((BLK, BLK), F32),
-        pltpu.VMEM((BLK, heads * BLK), BF16),
-        pltpu.VMEM((BLK, heads * BLK), BF16),
+        pltpu.VMEM((2 * BLK, BLK), F32),
+        pltpu.VMEM((2 * BLK, heads * BLK), BF16),
+        pltpu.VMEM((2 * BLK, heads * BLK), BF16),
         pltpu.VMEM((D_HEAD, heads * BLK), F32),
         pltpu.VMEM(total, BF16),
         pltpu.VMEM((chunks,) + pairs[0].shape, BF16),
@@ -290,7 +295,7 @@
         operands.append(earlier)
         specs.append(HBM)
         outs += [jax.ShapeDtypeStruct((rows, total[1]), kind) for rows, kind in ends]
-        scratch += [pltpu.VMEM(total, F32), pltpu.VMEM(total, F32), pltpu.SemaphoreType.DMA]
+        scratch += [pltpu.VMEM(total, F32), pltpu.SemaphoreType.DMA]
     else:
         outs.append(jax.ShapeDtypeStruct(total, F32))
     results = pl.pallas_call(

time: 156 us -> 147 us (0.942)
  Pallas kernels: 44.1 us -> 39.3 us
  waiting for transfers between devices: 42.9 us -> 39.3 us
    pallas_call x2, Pallas kernels: 30.4 us -> 25.6 us  [run_pairs(): pl.pallas_call(functools.partial(pair_kernel, chunks, places, ends, heads...]
    ppermute x4, waiting for transfers between devices: 15.3 us -> 11.7 us  [body(): come[m] = lax.ppermute(piece, 'ctx', moves)]
  transfers between devices with their start and end apart: 22 -> 22, of which waited for: 10 -> 10; matrix products, arithmetic and copies ran while one was open for 14% -> 14% of each run, Pallas kernels for 20% -> 19%
where the time goes in v1:
time: 147 us; the launch traced here: 145 us
  starting transfers between devices  40.6 us (28%)
  Pallas kernels  39.3 us (27%)
  waiting for transfers between devices  39.3 us (27%)
  local copies, waits for them, and re-layouts  15.7 us (11%)
  other arithmetic  8.86 us (6%)
    pallas_call x2, Pallas kernels, run_pairs(): pl.pallas_call(functools.partial(pair_kernel, chunks, places, ends, heads...  25.6 us
    ppermute x12, waiting for transfers between devices, swap(): return lax.ppermute(value, 'ctx', [(s, s ^ mask) for s in range(count)])  20.3 us
    ppermute x6, starting transfers between devices, shift(): return lax.ppermute(value, 'ctx', moves)  17.7 us
    ppermute x12, starting transfers between devices, swap(): return lax.ppermute(value, 'ctx', [(s, s ^ mask) for s in range(count)])  15.1 us
    ppermute x4, waiting for transfers between devices, body(): come[m] = lax.ppermute(piece, 'ctx', moves)  11.7 us
    pallas_call x4, Pallas kernels, pack_pair(): pl.pallas_call(functools.partial(pair_pack_kernel, heads), out_shape=jax....  9.83 us
    ppermute x4, starting transfers between devices, body(): come[m] = lax.ppermute(piece, 'ctx', moves)  7.76 us
    ppermute x6, waiting for transfers between devices, shift(): return lax.ppermute(value, 'ctx', moves)  7.32 us
  transfers between devices with their start and end apart: 22, of which 10 were waited for; matrix products, arithmetic and copies ran while one was open for 14% of the time, Pallas kernels for 19%

profile of v1, /device:TPU:14, one launch (start us, length us, event | category | flops | bytes accessed | tf_op | source)
XLA Modules:
  0.0 144.7 jit_solution(15103112889570427722)
XLA Ops:
  0.6 1.9 %shard_map.103 = (bf16[272,256]{1,0:T(8,128)(2,1)}, bf16[272,256]{1,0:T(8,128)(2,1)}, bf16[272,256]{1,0:T(8,128)(2,1)}, bf16[272,256]{1,0:T(8,128)(2,1)}) custom-call(s32[1]{0:T(128)} %bitcast.me_ref.group_ref, bf16[256,512]{1,0:T(8,128)(2,1)} %key_ref.1, bf16[256,512]{1,0:T(8,128)(2,1)} %value_ref.1, s32[2,16]{1,0:T(2,128)} %active_ref.1), custom_call_target="tpu_custom_call" | custom-call | tf_op jit(solution)/shard_map/pallas_call | solution.py:44
  3.1 1.5 %collective-permute-start.2 = (bf16[272,256]{1,0:T(8,128)(2,1)}, bf16[272,256]{1,0:T(8,128)(2,1)}, u32[]{:S(2)}, u32[]{:S(2)}) collective-permute-start(bf16[272,256]{1,0:T(8,128)(2,1)} %get-tuple-element.27), channel_id=1, source_target_pairs={{0,6},{2,4},{4,2},{6,0},{8,14},{10,12},{12,10},{14,8},{16,22},{18,... | collective-permute-start | bytes 417800 | tf_op jit(solution)/shard_map/ppermute | solution.py:367
  4.6 1.5 %collective-permute-start = (bf16[272,256]{1,0:T(8,128)(2,1)}, bf16[272,256]{1,0:T(8,128)(2,1)}, u32[]{:S(2)}, u32[]{:S(2)}) collective-permute-start(bf16[272,256]{1,0:T(8,128)(2,1)} %get-tuple-element.25), channel_id=1, source_target_pairs={{0,2},{2,0},{4,6},{6,4},{8,10},{10,8},{12,14},{14,12},{16,18},{18,... | collective-permute-start | bytes 417800 | tf_op jit(solution)/shard_map/ppermute | solution.py:367
  6.1 2.5 %shard_map.106 = bf16[2,264,1024]{2,1,0:T(8,128)(2,1)} custom-call(s32[1]{0:T(128)} %bitcast.6.group_ref, bf16[256,4096]{1,0:T(8,128)(2,1)} %query_ref.7, bf16[256,4096]{1,0:T(8,128)(2,1)} %grad_ref.7, bf16[256,4096]{1,0:T(8,128)(2,1)} %fwd_ref.7, f32[32,256]{1,0:T(8,128)} %log_ref.7), custom_call_target="tpu_custom_call" | custom-call | tf_op jit(solution)/shard_map/pallas_call | solution.py:81
  9.0 2.4 %shard_map.107 = bf16[2,264,1024]{2,1,0:T(8,128)(2,1)} custom-call(s32[1]{0:T(128)} %bitcast.7.group_ref, bf16[256,4096]{1,0:T(8,128)(2,1)} %query_ref.7, bf16[256,4096]{1,0:T(8,128)(2,1)} %grad_ref.7, bf16[256,4096]{1,0:T(8,128)(2,1)} %fwd_ref.7, f32[32,256]{1,0:T(8,128)} %log_ref.7), custom_call_target="tpu_custom_call" | custom-call | tf_op jit(solution)/shard_map/pallas_call | solution.py:81
  14.6 2.8 %convert_reduce_fusion = s32[1024]{0:T(1024)S(1)} fusion(s32[1024]{0:T(1024)S(1)} %bitcast.20, s32[4096]{0:T(1024)} %param.14), kind=kLoop, calls=%fused_computation.3 | loop fusion | flops 12581888 | bytes 24576 | tf_op jit(solution)/shard_map/reduce_sum | solution.py:346
  18.1 1.6 %slice_reduce_fusion = (s32[32]{0:T(128)}, s32[32]{0:T(128)}) fusion(s32[32,128]{1,0:T(8,128)} %bitcast.18), kind=kLoop, calls=%fused_computation.10 | loop fusion | bytes 512 | tf_op jit(solution)/shard_map/slice | solution.py:326
  20.3 2.5 %shard_map.105.refs_2_ = bf16[2,264,1024]{2,1,0:T(8,128)(2,1)} custom-call(s32[1]{0:T(128)} %bitcast.me_ref.group_ref, bf16[256,4096]{1,0:T(8,128)(2,1)} %query_ref.7, bf16[256,4096]{1,0:T(8,128)(2,1)} %grad_ref.7, bf16[256,4096]{1,0:T(8,128)(2,1)} %fwd_ref.7, f32[32,256]{1,0:T(8,128)} %log_ref.7), custom_call_target="tpu_custom_call" | custom-call | tf_op jit(solution)/shard_map/pallas_call | solution.py:81
  30.0 2.5 %shard_map.104 = bf16[2,264,1024]{2,1,0:T(8,128)(2,1)} custom-call(s32[1]{0:T(128)} %bitcast.3.group_ref, bf16[256,4096]{1,0:T(8,128)(2,1)} %query_ref.7, bf16[256,4096]{1,0:T(8,128)(2,1)} %grad_ref.7, bf16[256,4096]{1,0:T(8,128)(2,1)} %fwd_ref.7, f32[32,256]{1,0:T(8,128)} %log_ref.7), custom_call_target="tpu_custom_call" | custom-call | tf_op jit(solution)/shard_map/pallas_call | solution.py:81
  32.5 2.4 %collective-permute-start.3 = (bf16[2,264,1024]{2,1,0:T(8,128)(2,1)}, bf16[2,264,1024]{2,1,0:T(8,128)(2,1)S(1)}, u32[]{:S(2)}, u32[]{:S(2)}) collective-permute-start(bf16[2,264,1024]{2,1,0:T(8,128)(2,1)} %shard_map.104), channel_id=1, source_target_pairs={{0,6},{2,4},{4,2},{6,0},{8,14},{10,12},{12,10},{14,8},{16,22},{18,... | collective-permute-start | bytes 3244040 | tf_op jit(solution)/shard_map/ppermute | solution.py:367
  35.9 3.5 %collective-permute-start.6 = (bf16[544,256]{1,0:T(8,128)(2,1)S(1)}, bf16[544,256]{1,0:T(8,128)(2,1)S(1)}, u32[]{:S(2)}, u32[]{:S(2)}) collective-permute-start(bf16[544,256]{1,0:T(8,128)(2,1)S(1)} %pad_maximum_fusion.1), channel_id=1, source_target_pairs={{0,8},{2,10},{4,12},{6,14},{8,16},{10,18},{12,20},{14,22},{16,24},... | collective-permute-start | bytes 835592 | tf_op jit(solution)/shard_map/ppermute | solution.py:371
  40.4 3.5 %collective-permute-start.4 = (bf16[544,256]{1,0:T(8,128)(2,1)S(1)}, bf16[544,256]{1,0:T(8,128)(2,1)S(1)}, u32[]{:S(2)}, u32[]{:S(2)}) collective-permute-start(bf16[544,256]{1,0:T(8,128)(2,1)S(1)} %pad_maximum_fusion), channel_id=1, source_target_pairs={{0,8},{2,10},{4,12},{6,14},{8,16},{10,18},{12,20},{14,22},{16,24},... | collective-permute-start | bytes 835592 | tf_op jit(solution)/shard_map/ppermute | solution.py:371
  46.7 3.2 %collective-permute-start.7 = (bf16[544,256]{1,0:T(8,128)(2,1)S(1)}, bf16[544,256]{1,0:T(8,128)(2,1)S(1)}, u32[]{:S(2)}, u32[]{:S(2)}) collective-permute-start(bf16[544,256]{1,0:T(8,128)(2,1)S(1)} %collective-permute-done.6.refs_9_.refs_7_), channel_id=1, source_target_pairs={{0,8},{2,10},{4,12},{6,14},{8,16},{10,18},{12,20},{14,22},{16,24},... | collective-permute-start | bytes 835592 | tf_op jit(solution)/shard_map/ppermute | solution.py:371
  49.9 2.3 %collective-permute-done.4.refs_8_.refs_6_ = bf16[544,256]{1,0:T(8,128)(2,1)S(1)} collective-permute-done((bf16[544,256]{1,0:T(8,128)(2,1)S(1)}, bf16[544,256]{1,0:T(8,128)(2,1)S(1)}, u32[]{:S(2)}, u32[]{:S(2)}) %collective-permute-start.4) | collective-permute-done | bytes 278560 | tf_op jit(solution)/shard_map/ppermute | solution.py:371
  52.3 3.6 %collective-permute-start.5 = (bf16[544,256]{1,0:T(8,128)(2,1)S(1)}, bf16[544,256]{1,0:T(8,128)(2,1)S(1)}, u32[]{:S(2)}, u32[]{:S(2)}) collective-permute-start(bf16[544,256]{1,0:T(8,128)(2,1)S(1)} %collective-permute-done.4.refs_8_.refs_6_), channel_id=1, source_target_pairs={{0,8},{2,10},{4,12},{6,14},{8,16},{10,18},{12,20},{14,22},{16,24},... | collective-permute-start | bytes 835592 | tf_op jit(solution)/shard_map/ppermute | solution.py:371
  58.2 4.2 %collective-permute-done.5.refs_6_.refs_4_ = bf16[544,256]{1,0:T(8,128)(2,1)S(1)} collective-permute-done((bf16[544,256]{1,0:T(8,128)(2,1)S(1)}, bf16[544,256]{1,0:T(8,128)(2,1)S(1)}, u32[]{:S(2)}, u32[]{:S(2)}) %collective-permute-start.5) | collective-permute-done | bytes 278560 | tf_op jit(solution)/shard_map/ppermute | solution.py:371
  65.3 17.4 %shard_map.108 = (bf16[256,1024]{1,0:T(8,128)(2,1)S(1)}, bf16[256,1024]{1,0:T(8,128)(2,1)S(1)}, bf16[256,1024]{1,0:T(8,128)(2,1)S(1)}, f32[3072,256]{1,0:T(8,128)S(1)}) custom-call(s32[6]{0:T(128)S(1)} %bitcast.16, s32[96]{0:T(128)S(1)} %reshape.347.refs_1_, bf16[2,264,1024]{2,1,0:T(8,128)(2,1)S(1)} %copy-done, ...), custom_call_target="tpu_custom_call" | custom-call | flops 6039797760 | bytes 8388608 | tf_op jit(solution)/shard_map/pallas_call | solution.py:301
  82.7 8.2 %shard_map.109 = (bf16[256,1024]{1,0:T(8,128)(2,1)S(1)}, bf16[512,256]{1,0:T(8,128)(2,1)S(1)}, bf16[512,256]{1,0:T(8,128)(2,1)S(1)}, f32[512,256]{1,0:T(8,128)S(...) custom-call(s32[2]{0:T(128)S(1)} %slice.42.refs_0_, ...), custom_call_target="tpu_custom_call" | custom-call | flops 2013265920 | bytes 8388608 | tf_op jit(solution)/shard_map/pallas_call | solution.py:301
  90.9 1.9 %collective-permute-start.16 = (bf16[512,256]{1,0:T(8,128)(2,1)S(1)}, bf16[512,256]{1,0:T(8,128)(2,1)S(1)}, u32[]{:S(2)}, u32[]{:S(2)}) collective-permute-start(bf16[512,256]{1,0:T(8,128)(2,1)S(1)} %get-tuple-element.38), channel_id=1, source_target_pairs={{8,0},{10,2},{12,4},{14,6},{16,8},{18,10},{20,12},{22,14},{24,16},... | collective-permute-start | bytes 786440 | tf_op jit(solution)/shard_map/ppermute | solution.py:371
  94.0 1.9 %collective-permute-start.13 = (bf16[512,256]{1,0:T(8,128)(2,1)S(1)}, bf16[512,256]{1,0:T(8,128)(2,1)S(1)}, u32[]{:S(2)}, u32[]{:S(2)}) collective-permute-start(bf16[512,256]{1,0:T(8,128)(2,1)S(1)} %get-tuple-element.34), channel_id=1, source_target_pairs={{8,0},{10,2},{12,4},{14,6},{16,8},{18,10},{20,12},{22,14},{24,16},... | collective-permute-start | bytes 786440 | tf_op jit(solution)/shard_map/ppermute | solution.py:371
  95.9 2.5 %collective-permute-start.21 = (bf16[256,1024]{1,0:T(8,128)(2,1)S(1)}, bf16[256,1024]{1,0:T(8,128)(2,1)S(1)}, u32[]{:S(2)}, u32[]{:S(2)}) collective-permute-start(bf16[256,1024]{1,0:T(8,128)(2,1)S(1)} %get-tuple-element.44), channel_id=1, source_target_pairs={{0,6},{2,4},{4,2},{6,0},{8,14},{10,12},{12,10},{14,8},{16,22},{18,... | collective-permute-start | bytes 1572872 | tf_op jit(solution)/shard_map/ppermute | solution.py:367
  99.0 9.8 %collective-permute-done.11.refs_2_ = bf16[256,256]{1,0:T(8,128)(2,1)S(1)} collective-permute-done((bf16[256,256]{1,0:T(8,128)(2,1)S(1)}, bf16[256,256]{1,0:T(8,128)(2,1)S(1)}, u32[]{:S(2)}, u32[]{:S(2)}) %collective-permute-start.11) | collective-permute-done | bytes 131104 | tf_op jit(solution)/shard_map/ppermute | solution.py:367
  108.7 4.0 %collective-permute-start.12 = (bf16[256,256]{1,0:T(8,128)(2,1)S(1)}, bf16[256,256]{1,0:T(8,128)(2,1)S(1)}, u32[]{:S(2)}, u32[]{:S(2)}) collective-permute-start(bf16[256,256]{1,0:T(8,128)(2,1)S(1)} %get-tuple-element.32), channel_id=1, source_target_pairs={{0,6},{2,4},{4,2},{6,0},{8,14},{10,12},{12,10},{14,8},{16,22},{18,... | collective-permute-start | bytes 393224 | tf_op jit(solution)/shard_map/ppermute | solution.py:367
  112.8 10.4 %collective-permute-done.12.refs_3_ = bf16[256,256]{1,0:T(8,128)(2,1)S(1)} collective-permute-done((bf16[256,256]{1,0:T(8,128)(2,1)S(1)}, bf16[256,256]{1,0:T(8,128)(2,1)S(1)}, u32[]{:S(2)}, u32[]{:S(2)}) %collective-permute-start.12) | collective-permute-done | bytes 131104 | tf_op jit(solution)/shard_map/ppermute | solution.py:367
  123.3 1.9 %collective-permute-start.17 = (bf16[256,256]{1,0:T(8,128)(2,1)S(1)}, bf16[256,256]{1,0:T(8,128)(2,1)S(1)}, u32[]{:S(2)}, u32[]{:S(2)}) collective-permute-start(bf16[256,256]{1,0:T(8,128)(2,1)S(1)} %get-tuple-element.39), channel_id=1, source_target_pairs={{8,4},{10,6},{12,0},{14,2},{16,12},{18,14},{20,8},{22,10},{24,20},... | collective-permute-start | bytes 393224 | tf_op jit(solution)/shard_map/ppermute | solution.py:434
  125.2 1.9 %collective-permute-start.18 = (bf16[256,256]{1,0:T(8,128)(2,1)S(1)}, bf16[256,256]{1,0:T(8,128)(2,1)S(1)}, u32[]{:S(2)}, u32[]{:S(2)}) collective-permute-start(bf16[256,256]{1,0:T(8,128)(2,1)S(1)} %get-tuple-element.40), channel_id=1, source_target_pairs={{8,6},{10,4},{12,2},{14,0},{16,14},{18,12},{20,10},{22,8},{24,22},... | collective-permute-start | bytes 393224 | tf_op jit(solution)/shard_map/ppermute | solution.py:434
  127.2 4.3 %collective-permute-done.17.refs_6_ = bf16[256,256]{1,0:T(8,128)(2,1)S(1)} collective-permute-done((bf16[256,256]{1,0:T(8,128)(2,1)S(1)}, bf16[256,256]{1,0:T(8,128)(2,1)S(1)}, u32[]{:S(2)}, u32[]{:S(2)}) %collective-permute-start.17) | collective-permute-done | bytes 131104 | tf_op jit(solution)/shard_map/ppermute | solution.py:434
  131.5 1.9 %collective-permute-start.14 = (bf16[256,256]{1,0:T(8,128)(2,1)S(1)}, bf16[256,256]{1,0:T(8,128)(2,1)S(1)}, u32[]{:S(2)}, u32[]{:S(2)}) collective-permute-start(bf16[256,256]{1,0:T(8,128)(2,1)S(1)} %get-tuple-element.35), channel_id=1, source_target_pairs={{8,0},{10,2},{12,4},{14,6},{16,8},{18,10},{20,12},{22,14},{24,16},... | collective-permute-start | bytes 393224 | tf_op jit(solution)/shard_map/ppermute | solution.py:434
  133.9 2.0 %collective-permute-start.15 = (bf16[256,256]{1,0:T(8,128)(2,1)S(1)}, bf16[256,256]{1,0:T(8,128)(2,1)S(1)}, u32[]{:S(2)}, u32[]{:S(2)}) collective-permute-start(bf16[256,256]{1,0:T(8,128)(2,1)S(1)} %get-tuple-element.36), channel_id=1, source_target_pairs={{8,2},{10,0},{12,6},{14,4},{16,10},{18,8},{20,14},{22,12},{24,18},... | collective-permute-start | bytes 393224 | tf_op jit(solution)/shard_map/ppermute | solution.py:434
  135.9 3.7 %collective-permute-done.14.refs_4_ = bf16[256,256]{1,0:T(8,128)(2,1)S(1)} collective-permute-done((bf16[256,256]{1,0:T(8,128)(2,1)S(1)}, bf16[256,256]{1,0:T(8,128)(2,1)S(1)}, u32[]{:S(2)}, u32[]{:S(2)}) %collective-permute-start.14) | collective-permute-done | bytes 131104 | tf_op jit(solution)/shard_map/ppermute | solution.py:434
  139.6 3.2 %collective-permute-done.15.refs_5_ = bf16[256,256]{1,0:T(8,128)(2,1)S(1)} collective-permute-done((bf16[256,256]{1,0:T(8,128)(2,1)S(1)}, bf16[256,256]{1,0:T(8,128)(2,1)S(1)}, u32[]{:S(2)}, u32[]{:S(2)}) %collective-permute-start.15) | collective-permute-done | bytes 131104 | tf_op jit(solution)/shard_map/ppermute | solution.py:434
  142.8 1.8 %shard_map.112 = (bf16[256,4096]{1,0:T(8,128)(2,1)}, bf16[256,512]{1,0:T(8,128)(2,1)}, bf16[256,512]{1,0:T(8,128)(2,1)}) custom-call(s32[1]{0:T(128)} %bitcast.me_ref.group_ref, f32[256,256]{1,0:T(8,128)S(1)} %get-tuple-element.29.refs_0_, bf16[256,256]{1,0:T(8,128)(2,1)S(1)} %collective-permute-done.10.refs_1_, ...), custom_call_target="tpu_custom_call" | custom-call | tf_op jit(solution)/shard_map/pallas_call | solution.py:130
  (75 shorter events, 24.8 us)
Async XLA Ops:
  2.6 29.9 %collective-permute-start.1 = (bf16[272,256]{1,0:T(8,128)(2,1)}, bf16[272,256]{1,0:T(8,128)(2,1)}, u32[]{:S(2)}, u32[]{:S(2)}) collective-permute-start(bf16[272,256]{1,0:T(8,128)(2,1)} %get-tuple-element.26), channel_id=1, source_target_pairs={{0,4},{2,6},{4,0},{6,2},{8,12},{10,14},{12,8},{14,10},{16,20},{18,... | collective-permute-start | bytes 417800 | tf_op jit(solution)/shard_map/ppermute | solution.py:367
  3.1 31.9 %collective-permute-start.2 = (bf16[272,256]{1,0:T(8,128)(2,1)}, bf16[272,256]{1,0:T(8,128)(2,1)}, u32[]{:S(2)}, u32[]{:S(2)}) collective-permute-start(bf16[272,256]{1,0:T(8,128)(2,1)} %get-tuple-element.27), channel_id=1, source_target_pairs={{0,6},{2,4},{4,2},{6,0},{8,14},{10,12},{12,10},{14,8},{16,22},{18,... | collective-permute-start | bytes 417800 | tf_op jit(solution)/shard_map/ppermute | solution.py:367
  4.6 34.9 %collective-permute-start = (bf16[272,256]{1,0:T(8,128)(2,1)}, bf16[272,256]{1,0:T(8,128)(2,1)}, u32[]{:S(2)}, u32[]{:S(2)}) collective-permute-start(bf16[272,256]{1,0:T(8,128)(2,1)} %get-tuple-element.25), channel_id=1, source_target_pairs={{0,2},{2,0},{4,6},{6,4},{8,10},{10,8},{12,14},{14,12},{16,18},{18,... | collective-permute-start | bytes 417800 | tf_op jit(solution)/shard_map/ppermute | solution.py:367
  8.5 53.9 %collective-permute-start.8 = (bf16[2,264,1024]{2,1,0:T(8,128)(2,1)}, bf16[2,264,1024]{2,1,0:T(8,128)(2,1)}, u32[]{:S(2)}, u32[]{:S(2)}) collective-permute-start(bf16[2,264,1024]{2,1,0:T(8,128)(2,1)} %shard_map.106), channel_id=1, source_target_pairs={{0,2},{2,0},{4,6},{6,4},{8,10},{10,8},{12,14},{14,12},{16,18},{18,... | collective-permute-start | bytes 3244040 | tf_op jit(solution)/shard_map/ppermute | solution.py:367
  11.5 51.0 %collective-permute-start.9 = (bf16[2,264,1024]{2,1,0:T(8,128)(2,1)}, bf16[2,264,1024]{2,1,0:T(8,128)(2,1)}, u32[]{:S(2)}, u32[]{:S(2)}) collective-permute-start(bf16[2,264,1024]{2,1,0:T(8,128)(2,1)} %shard_map.107), channel_id=1, source_target_pairs={{0,4},{2,6},{4,0},{6,2},{8,12},{10,14},{12,8},{14,10},{16,20},{18,... | collective-permute-start | bytes 3244040 | tf_op jit(solution)/shard_map/ppermute | solution.py:367
  12.7 0.5 copy-start.8
  13.3 6.5 %copy-start.7 = (s32[1024]{0:T(1024)}, s32[1024]{0:T(1024)S(1)}, u32[]{:S(2)}) copy-start(s32[1024]{0:T(1024)S(1)} %pad_clamp_fusion) | copy-start | bytes 12292
  22.8 0.7 copy-start.4
  23.5 2.2 %copy-start.5 = (s32[32]{0:T(128)S(1)}, s32[32]{0:T(128)}, u32[]{:S(2)}) copy-start(s32[32]{0:T(128)} %get-tuple-element.45) | copy-start | bytes 388
  23.5 4.7 %copy-start.6 = (s32[4,2]{1,0:T(4,128)S(1)}, s32[4,2]{1,0:T(4,128)}, u32[]{:S(2)}) copy-start(s32[4,2]{1,0:T(4,128)} %get-tuple-element.49) | copy-start | bytes 100
  32.5 50.2 %collective-permute-start.3 = (bf16[2,264,1024]{2,1,0:T(8,128)(2,1)}, bf16[2,264,1024]{2,1,0:T(8,128)(2,1)S(1)}, u32[]{:S(2)}, u32[]{:S(2)}) collective-permute-start(bf16[2,264,1024]{2,1,0:T(8,128)(2,1)} %shard_map.104), channel_id=1, source_target_pairs={{0,6},{2,4},{4,2},{6,0},{8,14},{10,12},{12,10},{14,8},{16,22},{18,... | collective-permute-start | bytes 3244040 | tf_op jit(solution)/shard_map/ppermute | solution.py:367
  35.9 10.7 %collective-permute-start.6 = (bf16[544,256]{1,0:T(8,128)(2,1)S(1)}, bf16[544,256]{1,0:T(8,128)(2,1)S(1)}, u32[]{:S(2)}, u32[]{:S(2)}) collective-permute-start(bf16[544,256]{1,0:T(8,128)(2,1)S(1)} %pad_maximum_fusion.1), channel_id=1, source_target_pairs={{0,8},{2,10},{4,12},{6,14},{8,16},{10,18},{12,20},{14,22},{16,24},... | collective-permute-start | bytes 835592 | tf_op jit(solution)/shard_map/ppermute | solution.py:371
  40.4 11.8 %collective-permute-start.4 = (bf16[544,256]{1,0:T(8,128)(2,1)S(1)}, bf16[544,256]{1,0:T(8,128)(2,1)S(1)}, u32[]{:S(2)}, u32[]{:S(2)}) collective-permute-start(bf16[544,256]{1,0:T(8,128)(2,1)S(1)} %pad_maximum_fusion), channel_id=1, source_target_pairs={{0,8},{2,10},{4,12},{6,14},{8,16},{10,18},{12,20},{14,22},{16,24},... | collective-permute-start | bytes 835592 | tf_op jit(solution)/shard_map/ppermute | solution.py:371
  46.7 11.5 %collective-permute-start.7 = (bf16[544,256]{1,0:T(8,128)(2,1)S(1)}, bf16[544,256]{1,0:T(8,128)(2,1)S(1)}, u32[]{:S(2)}, u32[]{:S(2)}) collective-permute-start(bf16[544,256]{1,0:T(8,128)(2,1)S(1)} %collective-permute-done.6.refs_9_.refs_7_), channel_id=1, source_target_pairs={{0,8},{2,10},{4,12},{6,14},{8,16},{10,18},{12,20},{14,22},{16,24},... | collective-permute-start | bytes 835592 | tf_op jit(solution)/shard_map/ppermute | solution.py:371
  52.3 10.2 %collective-permute-start.5 = (bf16[544,256]{1,0:T(8,128)(2,1)S(1)}, bf16[544,256]{1,0:T(8,128)(2,1)S(1)}, u32[]{:S(2)}, u32[]{:S(2)}) collective-permute-start(bf16[544,256]{1,0:T(8,128)(2,1)S(1)} %collective-permute-done.4.refs_8_.refs_6_), channel_id=1, source_target_pairs={{0,8},{2,10},{4,12},{6,14},{8,16},{10,18},{12,20},{14,22},{16,24},... | collective-permute-start | bytes 835592 | tf_op jit(solution)/shard_map/ppermute | solution.py:371
  62.5 1.2 copy-start
  63.7 0.9 copy-start.1
  64.6 0.7 copy-start.2
  65.3 17.4 %copy-start.3 = (s32[2,128]{1,0:T(2,128)S(1)}, s32[2,128]{1,0:T(2,128)}, u32[]{:S(2)}) copy-start(s32[2,128]{1,0:T(2,128)} %slice.44.refs_3_) | copy-start | bytes 3076
  90.9 17.8 %collective-permute-start.16 = (bf16[512,256]{1,0:T(8,128)(2,1)S(1)}, bf16[512,256]{1,0:T(8,128)(2,1)S(1)}, u32[]{:S(2)}, u32[]{:S(2)}) collective-permute-start(bf16[512,256]{1,0:T(8,128)(2,1)S(1)} %get-tuple-element.38), channel_id=1, source_target_pairs={{8,0},{10,2},{12,4},{14,6},{16,8},{18,10},{20,12},{22,14},{24,16},... | collective-permute-start | bytes 786440 | tf_op jit(solution)/shard_map/ppermute | solution.py:371
  92.9 5.6 %collective-permute-start.10 = (bf16[256,256]{1,0:T(8,128)(2,1)S(1)}, bf16[256,256]{1,0:T(8,128)(2,1)S(1)}, u32[]{:S(2)}, u32[]{:S(2)}) collective-permute-start(bf16[256,256]{1,0:T(8,128)(2,1)S(1)} %get-tuple-element.30), channel_id=1, source_target_pairs={{0,2},{2,0},{4,6},{6,4},{8,10},{10,8},{12,14},{14,12},{16,18},{18,... | collective-permute-start | bytes 393224 | tf_op jit(solution)/shard_map/ppermute | solution.py:367
  93.5 15.2 %collective-permute-start.11 = (bf16[256,256]{1,0:T(8,128)(2,1)S(1)}, bf16[256,256]{1,0:T(8,128)(2,1)S(1)}, u32[]{:S(2)}, u32[]{:S(2)}) collective-permute-start(bf16[256,256]{1,0:T(8,128)(2,1)S(1)} %get-tuple-element.31), channel_id=1, source_target_pairs={{0,4},{2,6},{4,0},{6,2},{8,12},{10,14},{12,8},{14,10},{16,20},{18,... | collective-permute-start | bytes 393224 | tf_op jit(solution)/shard_map/ppermute | solution.py:367
  94.0 31.2 %collective-permute-start.13 = (bf16[512,256]{1,0:T(8,128)(2,1)S(1)}, bf16[512,256]{1,0:T(8,128)(2,1)S(1)}, u32[]{:S(2)}, u32[]{:S(2)}) collective-permute-start(bf16[512,256]{1,0:T(8,128)(2,1)S(1)} %get-tuple-element.34), channel_id=1, source_target_pairs={{8,0},{10,2},{12,4},{14,6},{16,8},{18,10},{20,12},{22,14},{24,16},... | collective-permute-start | bytes 786440 | tf_op jit(solution)/shard_map/ppermute | solution.py:371
  95.9 46.9 %collective-permute-start.21 = (bf16[256,1024]{1,0:T(8,128)(2,1)S(1)}, bf16[256,1024]{1,0:T(8,128)(2,1)S(1)}, u32[]{:S(2)}, u32[]{:S(2)}) collective-permute-start(bf16[256,1024]{1,0:T(8,128)(2,1)S(1)} %get-tuple-element.44), channel_id=1, source_target_pairs={{0,6},{2,4},{4,2},{6,0},{8,14},{10,12},{12,10},{14,8},{16,22},{18,... | collective-permute-start | bytes 1572872 | tf_op jit(solution)/shard_map/ppermute | solution.py:367
  98.5 44.4 %collective-permute-start.19 = (bf16[256,1024]{1,0:T(8,128)(2,1)S(1)}, bf16[256,1024]{1,0:T(8,128)(2,1)S(1)}, u32[]{:S(2)}, u32[]{:S(2)}) collective-permute-start(bf16[256,1024]{1,0:T(8,128)(2,1)S(1)} %get-tuple-element.42), channel_id=1, source_target_pairs={{0,2},{2,0},{4,6},{6,4},{8,10},{10,8},{12,14},{14,12},{16,18},{18,... | collective-permute-start | bytes 1572872 | tf_op jit(solution)/shard_map/ppermute | solution.py:367
  108.7 34.1 %collective-permute-start.20 = (bf16[256,1024]{1,0:T(8,128)(2,1)S(1)}, bf16[256,1024]{1,0:T(8,128)(2,1)S(1)}, u32[]{:S(2)}, u32[]{:S(2)}) collective-permute-start(bf16[256,1024]{1,0:T(8,128)(2,1)S(1)} %get-tuple-element.43), channel_id=1, source_target_pairs={{0,4},{2,6},{4,0},{6,2},{8,12},{10,14},{12,8},{14,10},{16,20},{18,... | collective-permute-start | bytes 1572872 | tf_op jit(solution)/shard_map/ppermute | solution.py:367
  108.7 14.5 %collective-permute-start.12 = (bf16[256,256]{1,0:T(8,128)(2,1)S(1)}, bf16[256,256]{1,0:T(8,128)(2,1)S(1)}, u32[]{:S(2)}, u32[]{:S(2)}) collective-permute-start(bf16[256,256]{1,0:T(8,128)(2,1)S(1)} %get-tuple-element.32), channel_id=1, source_target_pairs={{0,6},{2,4},{4,2},{6,0},{8,14},{10,12},{12,10},{14,8},{16,22},{18,... | collective-permute-start | bytes 393224 | tf_op jit(solution)/shard_map/ppermute | solution.py:367
  123.3 8.2 %collective-permute-start.17 = (bf16[256,256]{1,0:T(8,128)(2,1)S(1)}, bf16[256,256]{1,0:T(8,128)(2,1)S(1)}, u32[]{:S(2)}, u32[]{:S(2)}) collective-permute-start(bf16[256,256]{1,0:T(8,128)(2,1)S(1)} %get-tuple-element.39), channel_id=1, source_target_pairs={{8,4},{10,6},{12,0},{14,2},{16,12},{18,14},{20,8},{22,10},{24,20},... | collective-permute-start | bytes 393224 | tf_op jit(solution)/shard_map/ppermute | solution.py:434
  125.2 8.7 %collective-permute-start.18 = (bf16[256,256]{1,0:T(8,128)(2,1)S(1)}, bf16[256,256]{1,0:T(8,128)(2,1)S(1)}, u32[]{:S(2)}, u32[]{:S(2)}) collective-permute-start(bf16[256,256]{1,0:T(8,128)(2,1)S(1)} %get-tuple-element.40), channel_id=1, source_target_pairs={{8,6},{10,4},{12,2},{14,0},{16,14},{18,12},{20,10},{22,8},{24,22},... | collective-permute-start | bytes 393224 | tf_op jit(solution)/shard_map/ppermute | solution.py:434
  131.5 8.1 %collective-permute-start.14 = (bf16[256,256]{1,0:T(8,128)(2,1)S(1)}, bf16[256,256]{1,0:T(8,128)(2,1)S(1)}, u32[]{:S(2)}, u32[]{:S(2)}) collective-permute-start(bf16[256,256]{1,0:T(8,128)(2,1)S(1)} %get-tuple-element.35), channel_id=1, source_target_pairs={{8,0},{10,2},{12,4},{14,6},{16,8},{18,10},{20,12},{22,14},{24,16},... | collective-permute-start | bytes 393224 | tf_op jit(solution)/shard_map/ppermute | solution.py:434
  133.9 8.9 %collective-permute-start.15 = (bf16[256,256]{1,0:T(8,128)(2,1)S(1)}, bf16[256,256]{1,0:T(8,128)(2,1)S(1)}, u32[]{:S(2)}, u32[]{:S(2)}) collective-permute-start(bf16[256,256]{1,0:T(8,128)(2,1)S(1)} %get-tuple-element.36), channel_id=1, source_target_pairs={{8,2},{10,0},{12,6},{14,4},{16,10},{18,8},{20,14},{22,12},{24,18},... | collective-permute-start | bytes 393224 | tf_op jit(solution)/shard_map/ppermute | solution.py:434

commit v2 on v1

--- a/solution.py
+++ b/solution.py
@@ -218,42 +218,46 @@
             query_at = lax.broadcasted_iota(jnp.int32, (BLK, BLK), 1)
             start_row = start_ref[pl.ds(row, 1), :]
 
-            def key_place(index):
-                code = list_ref[row * WINBLK + jnp.minimum(index, WINBLK - 1)]
-                distance = jnp.where(index < count_ref[row], code % WINBLK, -2)
-                there = key_at - distance * BLK
-                allowed = (there <= query_at) & (there >= start_row)
-                place = pl.ds(pl.multiple_of(code // WINBLK * BLK, BLK), BLK)
-                return place, jnp.where(allowed, 0.0, LOWEST)
-
-            def two_blocks(index, inner):
-                first, first_bias = key_place(2 * index)
-                second, second_bias = key_place(2 * index + 1)
-                bias_s[0:BLK, :] = first_bias
-                bias_s[BLK : 2 * BLK, :] = second_bias
-                key = jnp.concatenate([kv_s[first, 0:D_HEAD], kv_s[second, 0:D_HEAD]], axis=0)
+            def key_blocks(first, many):
+                places = []
+                for step in range(many):
+                    code = list_ref[row * WINBLK + first + step]
+                    there = key_at - code % WINBLK * BLK
+                    allowed = (there <= query_at) & (there >= start_row)
+                    bias_s[step * BLK : (step + 1) * BLK, :] = jnp.where(allowed, 0.0, LOWEST)
+                    places.append(pl.ds(pl.multiple_of(code // WINBLK * BLK, BLK), BLK))
+                used = pl.ds(0, many * BLK)
                 both = pl.ds(D_HEAD, D_HEAD)
-                value = jnp.concatenate([kv_s[first, both], kv_s[second, both]], axis=0)
+                key = jnp.concatenate([kv_s[at, 0:D_HEAD] for at in places], axis=0)
+                value = jnp.concatenate([kv_s[at, both] for at in places], axis=0)
                 for part_at in range(0, heads * BLK, wide):
                     span = pl.ds(part_at, wide)
                     score = lax.dot_general(key, q_s[span, :], NT, preferred_element_type=F32)
                     grad_w = lax.dot_general(value, g_s[span, :], NT, preferred_element_type=F32)
-                    bias = bias_s[...]
+                    bias = bias_s[used, :]
                     bias = jnp.concatenate([bias, bias], axis=1)
                     weight = jnp.exp2(score * (factor * LOG2E) + (bias - l_s[0:1, span]))
-                    p_s[:, span] = weight.astype(BF16)
-                    s_s[:, span] = (weight * (grad_w - t_s[0:1, span])).astype(BF16)
-                grads = s_s[...]
-                value_sum = jnp.dot(p_s[...], g_s[...], preferred_element_type=F32)
+                    p_s[used, span] = weight.astype(BF16)
+                    s_s[used, span] = (weight * (grad_w - t_s[0:1, span])).astype(BF16)
+                grads = s_s[used, :]
+                value_sum = jnp.dot(p_s[used, :], g_s[...], preferred_element_type=F32)
                 key_sum = jnp.dot(grads, q_s[...], preferred_element_type=F32)
-                sum_ref[first, D_HEAD : 2 * D_HEAD] += value_sum[0:BLK]
-                sum_ref[first, 0:D_HEAD] += key_sum[0:BLK]
-                sum_ref[second, D_HEAD : 2 * D_HEAD] += value_sum[BLK : 2 * BLK]
-                sum_ref[second, 0:D_HEAD] += key_sum[BLK : 2 * BLK]
+                for step, at in enumerate(places):
+                    sum_ref[at, both] += value_sum[step * BLK : (step + 1) * BLK]
+                    sum_ref[at, 0:D_HEAD] += key_sum[step * BLK : (step + 1) * BLK]
                 dq_s[...] += lax.dot_general(key, grads, TN, preferred_element_type=F32)
+
+            def two_blocks(index, inner):
+                key_blocks(2 * index, 2)
                 return inner
 
-            lax.fori_loop(0, (count_ref[row] + 1) // 2, two_blocks, 0)
+            found = count_ref[row]
+            lax.fori_loop(0, found // 2, two_blocks, 0)
+
+            @pl.when(found % 2 == 1)
+            def _():
+                key_blocks(found - 1, 1)
+
             for head in range(heads):
                 turned = jnp.transpose(dq_s[:, head * BLK : (head + 1) * BLK]) * factor
                 dq_refs[chunk][

time: 147 us -> 147 us (level)
  transfers between devices with their start and end apart: 22 -> 22, of which waited for: 10 -> 9; matrix products, arithmetic and copies ran while one was open for 14% -> 14% of each run, Pallas kernels for 19% -> 18%
where the time goes in v2:
time: 147 us; the launch traced here: 144 us
  starting transfers between devices  40.5 us (28%)
  waiting for transfers between devices  39.9 us (27%)
  Pallas kernels  38.5 us (26%)
  local copies, waits for them, and re-layouts  15.7 us (11%)
  other arithmetic  8.86 us (6%)
    pallas_call x2, Pallas kernels, run_pairs(): pl.pallas_call(functools.partial(pair_kernel, chunks, places, ends, heads...  24.8 us
    ppermute x12, waiting for transfers between devices, swap(): return lax.ppermute(value, 'ctx', [(s, s ^ mask) for s in range(count)])  20.4 us
    ppermute x6, starting transfers between devices, shift(): return lax.ppermute(value, 'ctx', moves)  17.7 us
    ppermute x12, starting transfers between devices, swap(): return lax.ppermute(value, 'ctx', [(s, s ^ mask) for s in range(count)])  15.1 us
    ppermute x4, waiting for transfers between devices, body(): come[m] = lax.ppermute(piece, 'ctx', moves)  12.2 us
    pallas_call x4, Pallas kernels, pack_pair(): pl.pallas_call(functools.partial(pair_pack_kernel, heads), out_shape=jax....  9.83 us
    ppermute x4, starting transfers between devices, body(): come[m] = lax.ppermute(piece, 'ctx', moves)  7.76 us
    ppermute x6, waiting for transfers between devices, shift(): return lax.ppermute(value, 'ctx', moves)  7.32 us
  transfers between devices with their start and end apart: 22, of which 9 were waited for; matrix products, arithmetic and copies ran while one was open for 14% of the time, Pallas kernels for 18%

profile of v2, /device:TPU:14, one launch (start us, length us, event | category | flops | bytes accessed | tf_op | source)
XLA Modules:
  0.0 144.4 jit_solution(1214023296993914043)
XLA Ops:
  0.6 1.9 %shard_map.103 = (bf16[272,256]{1,0:T(8,128)(2,1)}, bf16[272,256]{1,0:T(8,128)(2,1)}, bf16[272,256]{1,0:T(8,128)(2,1)}, bf16[272,256]{1,0:T(8,128)(2,1)}) custom-call(s32[1]{0:T(128)} %bitcast.me_ref.group_ref, bf16[256,512]{1,0:T(8,128)(2,1)} %key_ref.1, bf16[256,512]{1,0:T(8,128)(2,1)} %value_ref.1, s32[2,16]{1,0:T(2,128)} %active_ref.1), custom_call_target="tpu_custom_call" | custom-call | tf_op jit(solution)/shard_map/pallas_call | solution.py:44
  3.1 1.5 %collective-permute-start.2 = (bf16[272,256]{1,0:T(8,128)(2,1)}, bf16[272,256]{1,0:T(8,128)(2,1)}, u32[]{:S(2)}, u32[]{:S(2)}) collective-permute-start(bf16[272,256]{1,0:T(8,128)(2,1)} %get-tuple-element.27), channel_id=1, source_target_pairs={{0,6},{2,4},{4,2},{6,0},{8,14},{10,12},{12,10},{14,8},{16,22},{18,... | collective-permute-start | bytes 417800 | tf_op jit(solution)/shard_map/ppermute | solution.py:371
  4.6 1.5 %collective-permute-start = (bf16[272,256]{1,0:T(8,128)(2,1)}, bf16[272,256]{1,0:T(8,128)(2,1)}, u32[]{:S(2)}, u32[]{:S(2)}) collective-permute-start(bf16[272,256]{1,0:T(8,128)(2,1)} %get-tuple-element.25), channel_id=1, source_target_pairs={{0,2},{2,0},{4,6},{6,4},{8,10},{10,8},{12,14},{14,12},{16,18},{18,... | collective-permute-start | bytes 417800 | tf_op jit(solution)/shard_map/ppermute | solution.py:371
  6.1 2.5 %shard_map.106 = bf16[2,264,1024]{2,1,0:T(8,128)(2,1)} custom-call(s32[1]{0:T(128)} %bitcast.6.group_ref, bf16[256,4096]{1,0:T(8,128)(2,1)} %query_ref.7, bf16[256,4096]{1,0:T(8,128)(2,1)} %grad_ref.7, bf16[256,4096]{1,0:T(8,128)(2,1)} %fwd_ref.7, f32[32,256]{1,0:T(8,128)} %log_ref.7), custom_call_target="tpu_custom_call" | custom-call | tf_op jit(solution)/shard_map/pallas_call | solution.py:81
  9.0 2.4 %shard_map.107 = bf16[2,264,1024]{2,1,0:T(8,128)(2,1)} custom-call(s32[1]{0:T(128)} %bitcast.7.group_ref, bf16[256,4096]{1,0:T(8,128)(2,1)} %query_ref.7, bf16[256,4096]{1,0:T(8,128)(2,1)} %grad_ref.7, bf16[256,4096]{1,0:T(8,128)(2,1)} %fwd_ref.7, f32[32,256]{1,0:T(8,128)} %log_ref.7), custom_call_target="tpu_custom_call" | custom-call | tf_op jit(solution)/shard_map/pallas_call | solution.py:81
  14.6 2.8 %convert_reduce_fusion = s32[1024]{0:T(1024)S(1)} fusion(s32[1024]{0:T(1024)S(1)} %bitcast.20, s32[4096]{0:T(1024)} %param.14), kind=kLoop, calls=%fused_computation.3 | loop fusion | flops 12581888 | bytes 24576 | tf_op jit(solution)/shard_map/reduce_sum | solution.py:350
  18.1 1.6 %slice_reduce_fusion = (s32[32]{0:T(128)}, s32[32]{0:T(128)}) fusion(s32[32,128]{1,0:T(8,128)} %bitcast.18), kind=kLoop, calls=%fused_computation.10 | loop fusion | bytes 512 | tf_op jit(solution)/shard_map/slice | solution.py:330
  20.3 2.5 %shard_map.105.refs_2_ = bf16[2,264,1024]{2,1,0:T(8,128)(2,1)} custom-call(s32[1]{0:T(128)} %bitcast.me_ref.group_ref, bf16[256,4096]{1,0:T(8,128)(2,1)} %query_ref.7, bf16[256,4096]{1,0:T(8,128)(2,1)} %grad_ref.7, bf16[256,4096]{1,0:T(8,128)(2,1)} %fwd_ref.7, f32[32,256]{1,0:T(8,128)} %log_ref.7), custom_call_target="tpu_custom_call" | custom-call | tf_op jit(solution)/shard_map/pallas_call | solution.py:81
  30.0 2.5 %shard_map.104 = bf16[2,264,1024]{2,1,0:T(8,128)(2,1)} custom-call(s32[1]{0:T(128)} %bitcast.3.group_ref, bf16[256,4096]{1,0:T(8,128)(2,1)} %query_ref.7, bf16[256,4096]{1,0:T(8,128)(2,1)} %grad_ref.7, bf16[256,4096]{1,0:T(8,128)(2,1)} %fwd_ref.7, f32[32,256]{1,0:T(8,128)} %log_ref.7), custom_call_target="tpu_custom_call" | custom-call | tf_op jit(solution)/shard_map/pallas_call | solution.py:81
  32.5 2.4 %collective-permute-start.3 = (bf16[2,264,1024]{2,1,0:T(8,128)(2,1)}, bf16[2,264,1024]{2,1,0:T(8,128)(2,1)S(1)}, u32[]{:S(2)}, u32[]{:S(2)}) collective-permute-start(bf16[2,264,1024]{2,1,0:T(8,128)(2,1)} %shard_map.104), channel_id=1, source_target_pairs={{0,6},{2,4},{4,2},{6,0},{8,14},{10,12},{12,10},{14,8},{16,22},{18,... | collective-permute-start | bytes 3244040 | tf_op jit(solution)/shard_map/ppermute | solution.py:371
  35.9 3.5 %collective-permute-start.6 = (bf16[544,256]{1,0:T(8,128)(2,1)S(1)}, bf16[544,256]{1,0:T(8,128)(2,1)S(1)}, u32[]{:S(2)}, u32[]{:S(2)}) collective-permute-start(bf16[544,256]{1,0:T(8,128)(2,1)S(1)} %pad_maximum_fusion.1), channel_id=1, source_target_pairs={{0,8},{2,10},{4,12},{6,14},{8,16},{10,18},{12,20},{14,22},{16,24},... | collective-permute-start | bytes 835592 | tf_op jit(solution)/shard_map/ppermute | solution.py:375
  40.4 3.5 %collective-permute-start.4 = (bf16[544,256]{1,0:T(8,128)(2,1)S(1)}, bf16[544,256]{1,0:T(8,128)(2,1)S(1)}, u32[]{:S(2)}, u32[]{:S(2)}) collective-permute-start(bf16[544,256]{1,0:T(8,128)(2,1)S(1)} %pad_maximum_fusion), channel_id=1, source_target_pairs={{0,8},{2,10},{4,12},{6,14},{8,16},{10,18},{12,20},{14,22},{16,24},... | collective-permute-start | bytes 835592 | tf_op jit(solution)/shard_map/ppermute | solution.py:375
  46.7 3.2 %collective-permute-start.7 = (bf16[544,256]{1,0:T(8,128)(2,1)S(1)}, bf16[544,256]{1,0:T(8,128)(2,1)S(1)}, u32[]{:S(2)}, u32[]{:S(2)}) collective-permute-start(bf16[544,256]{1,0:T(8,128)(2,1)S(1)} %collective-permute-done.6.refs_9_.refs_7_), channel_id=1, source_target_pairs={{0,8},{2,10},{4,12},{6,14},{8,16},{10,18},{12,20},{14,22},{16,24},... | collective-permute-start | bytes 835592 | tf_op jit(solution)/shard_map/ppermute | solution.py:375
  49.9 2.3 %collective-permute-done.4.refs_8_.refs_6_ = bf16[544,256]{1,0:T(8,128)(2,1)S(1)} collective-permute-done((bf16[544,256]{1,0:T(8,128)(2,1)S(1)}, bf16[544,256]{1,0:T(8,128)(2,1)S(1)}, u32[]{:S(2)}, u32[]{:S(2)}) %collective-permute-start.4) | collective-permute-done | bytes 278560 | tf_op jit(solution)/shard_map/ppermute | solution.py:375
  52.3 3.6 %collective-permute-start.5 = (bf16[544,256]{1,0:T(8,128)(2,1)S(1)}, bf16[544,256]{1,0:T(8,128)(2,1)S(1)}, u32[]{:S(2)}, u32[]{:S(2)}) collective-permute-start(bf16[544,256]{1,0:T(8,128)(2,1)S(1)} %collective-permute-done.4.refs_8_.refs_6_), channel_id=1, source_target_pairs={{0,8},{2,10},{4,12},{6,14},{8,16},{10,18},{12,20},{14,22},{16,24},... | collective-permute-start | bytes 835592 | tf_op jit(solution)/shard_map/ppermute | solution.py:375
  58.2 4.2 %collective-permute-done.5.refs_6_.refs_4_ = bf16[544,256]{1,0:T(8,128)(2,1)S(1)} collective-permute-done((bf16[544,256]{1,0:T(8,128)(2,1)S(1)}, bf16[544,256]{1,0:T(8,128)(2,1)S(1)}, u32[]{:S(2)}, u32[]{:S(2)}) %collective-permute-start.5) | collective-permute-done | bytes 278560 | tf_op jit(solution)/shard_map/ppermute | solution.py:375
  65.3 16.7 %shard_map.108 = (bf16[256,1024]{1,0:T(8,128)(2,1)S(1)}, bf16[256,1024]{1,0:T(8,128)(2,1)S(1)}, bf16[256,1024]{1,0:T(8,128)(2,1)S(1)}, f32[3072,256]{1,0:T(8,128)S(1)}) custom-call(s32[6]{0:T(128)S(1)} %bitcast.16, s32[96]{0:T(128)S(1)} %reshape.347.refs_1_, bf16[2,264,1024]{2,1,0:T(8,128)(2,1)S(1)} %copy-done, ...), custom_call_target="tpu_custom_call" | custom-call | flops 6039797760 | bytes 8388608 | tf_op jit(solution)/shard_map/pallas_call | solution.py:305
  82.1 8.0 %shard_map.109 = (bf16[256,1024]{1,0:T(8,128)(2,1)S(1)}, bf16[512,256]{1,0:T(8,128)(2,1)S(1)}, bf16[512,256]{1,0:T(8,128)(2,1)S(1)}, f32[512,256]{1,0:T(8,128)S(...) custom-call(s32[2]{0:T(128)S(1)} %slice.42.refs_0_, ...), custom_call_target="tpu_custom_call" | custom-call | flops 2013265920 | bytes 8388608 | tf_op jit(solution)/shard_map/pallas_call | solution.py:305
  90.1 1.9 %collective-permute-start.16 = (bf16[512,256]{1,0:T(8,128)(2,1)S(1)}, bf16[512,256]{1,0:T(8,128)(2,1)S(1)}, u32[]{:S(2)}, u32[]{:S(2)}) collective-permute-start(bf16[512,256]{1,0:T(8,128)(2,1)S(1)} %get-tuple-element.38), channel_id=1, source_target_pairs={{8,0},{10,2},{12,4},{14,6},{16,8},{18,10},{20,12},{22,14},{24,16},... | collective-permute-start | bytes 786440 | tf_op jit(solution)/shard_map/ppermute | solution.py:375
  93.1 1.9 %collective-permute-start.13 = (bf16[512,256]{1,0:T(8,128)(2,1)S(1)}, bf16[512,256]{1,0:T(8,128)(2,1)S(1)}, u32[]{:S(2)}, u32[]{:S(2)}) collective-permute-start(bf16[512,256]{1,0:T(8,128)(2,1)S(1)} %get-tuple-element.34), channel_id=1, source_target_pairs={{8,0},{10,2},{12,4},{14,6},{16,8},{18,10},{20,12},{22,14},{24,16},... | collective-permute-start | bytes 786440 | tf_op jit(solution)/shard_map/ppermute | solution.py:375
  95.1 2.5 %collective-permute-start.21 = (bf16[256,1024]{1,0:T(8,128)(2,1)S(1)}, bf16[256,1024]{1,0:T(8,128)(2,1)S(1)}, u32[]{:S(2)}, u32[]{:S(2)}) collective-permute-start(bf16[256,1024]{1,0:T(8,128)(2,1)S(1)} %get-tuple-element.44), channel_id=1, source_target_pairs={{0,6},{2,4},{4,2},{6,0},{8,14},{10,12},{12,10},{14,8},{16,22},{18,... | collective-permute-start | bytes 1572872 | tf_op jit(solution)/shard_map/ppermute | solution.py:371
  98.1 9.8 %collective-permute-done.11.refs_2_ = bf16[256,256]{1,0:T(8,128)(2,1)S(1)} collective-permute-done((bf16[256,256]{1,0:T(8,128)(2,1)S(1)}, bf16[256,256]{1,0:T(8,128)(2,1)S(1)}, u32[]{:S(2)}, u32[]{:S(2)}) %collective-permute-start.11) | collective-permute-done | bytes 131104 | tf_op jit(solution)/shard_map/ppermute | solution.py:371
  107.9 3.9 %collective-permute-start.12 = (bf16[256,256]{1,0:T(8,128)(2,1)S(1)}, bf16[256,256]{1,0:T(8,128)(2,1)S(1)}, u32[]{:S(2)}, u32[]{:S(2)}) collective-permute-start(bf16[256,256]{1,0:T(8,128)(2,1)S(1)} %get-tuple-element.32), channel_id=1, source_target_pairs={{0,6},{2,4},{4,2},{6,0},{8,14},{10,12},{12,10},{14,8},{16,22},{18,... | collective-permute-start | bytes 393224 | tf_op jit(solution)/shard_map/ppermute | solution.py:371
  111.9 10.5 %collective-permute-done.12.refs_3_ = bf16[256,256]{1,0:T(8,128)(2,1)S(1)} collective-permute-done((bf16[256,256]{1,0:T(8,128)(2,1)S(1)}, bf16[256,256]{1,0:T(8,128)(2,1)S(1)}, u32[]{:S(2)}, u32[]{:S(2)}) %collective-permute-start.12) | collective-permute-done | bytes 131104 | tf_op jit(solution)/shard_map/ppermute | solution.py:371
  122.4 1.9 %collective-permute-start.17 = (bf16[256,256]{1,0:T(8,128)(2,1)S(1)}, bf16[256,256]{1,0:T(8,128)(2,1)S(1)}, u32[]{:S(2)}, u32[]{:S(2)}) collective-permute-start(bf16[256,256]{1,0:T(8,128)(2,1)S(1)} %get-tuple-element.39), channel_id=1, source_target_pairs={{8,4},{10,6},{12,0},{14,2},{16,12},{18,14},{20,8},{22,10},{24,20},... | collective-permute-start | bytes 393224 | tf_op jit(solution)/shard_map/ppermute | solution.py:438
  124.4 1.9 %collective-permute-start.18 = (bf16[256,256]{1,0:T(8,128)(2,1)S(1)}, bf16[256,256]{1,0:T(8,128)(2,1)S(1)}, u32[]{:S(2)}, u32[]{:S(2)}) collective-permute-start(bf16[256,256]{1,0:T(8,128)(2,1)S(1)} %get-tuple-element.40), channel_id=1, source_target_pairs={{8,6},{10,4},{12,2},{14,0},{16,14},{18,12},{20,10},{22,8},{24,22},... | collective-permute-start | bytes 393224 | tf_op jit(solution)/shard_map/ppermute | solution.py:438
  126.4 4.3 %collective-permute-done.17.refs_6_ = bf16[256,256]{1,0:T(8,128)(2,1)S(1)} collective-permute-done((bf16[256,256]{1,0:T(8,128)(2,1)S(1)}, bf16[256,256]{1,0:T(8,128)(2,1)S(1)}, u32[]{:S(2)}, u32[]{:S(2)}) %collective-permute-start.17) | collective-permute-done | bytes 131104 | tf_op jit(solution)/shard_map/ppermute | solution.py:438
  130.7 1.9 %collective-permute-start.14 = (bf16[256,256]{1,0:T(8,128)(2,1)S(1)}, bf16[256,256]{1,0:T(8,128)(2,1)S(1)}, u32[]{:S(2)}, u32[]{:S(2)}) collective-permute-start(bf16[256,256]{1,0:T(8,128)(2,1)S(1)} %get-tuple-element.35), channel_id=1, source_target_pairs={{8,0},{10,2},{12,4},{14,6},{16,8},{18,10},{20,12},{22,14},{24,16},... | collective-permute-start | bytes 393224 | tf_op jit(solution)/shard_map/ppermute | solution.py:438
  133.0 2.0 %collective-permute-start.15 = (bf16[256,256]{1,0:T(8,128)(2,1)S(1)}, bf16[256,256]{1,0:T(8,128)(2,1)S(1)}, u32[]{:S(2)}, u32[]{:S(2)}) collective-permute-start(bf16[256,256]{1,0:T(8,128)(2,1)S(1)} %get-tuple-element.36), channel_id=1, source_target_pairs={{8,2},{10,0},{12,6},{14,4},{16,10},{18,8},{20,14},{22,12},{24,18},... | collective-permute-start | bytes 393224 | tf_op jit(solution)/shard_map/ppermute | solution.py:438
  135.1 4.4 %collective-permute-done.14.refs_4_ = bf16[256,256]{1,0:T(8,128)(2,1)S(1)} collective-permute-done((bf16[256,256]{1,0:T(8,128)(2,1)S(1)}, bf16[256,256]{1,0:T(8,128)(2,1)S(1)}, u32[]{:S(2)}, u32[]{:S(2)}) %collective-permute-start.14) | collective-permute-done | bytes 131104 | tf_op jit(solution)/shard_map/ppermute | solution.py:438
  139.5 3.1 %collective-permute-done.15.refs_5_ = bf16[256,256]{1,0:T(8,128)(2,1)S(1)} collective-permute-done((bf16[256,256]{1,0:T(8,128)(2,1)S(1)}, bf16[256,256]{1,0:T(8,128)(2,1)S(1)}, u32[]{:S(2)}, u32[]{:S(2)}) %collective-permute-start.15) | collective-permute-done | bytes 131104 | tf_op jit(solution)/shard_map/ppermute | solution.py:438
  142.5 1.8 %shard_map.112 = (bf16[256,4096]{1,0:T(8,128)(2,1)}, bf16[256,512]{1,0:T(8,128)(2,1)}, bf16[256,512]{1,0:T(8,128)(2,1)}) custom-call(s32[1]{0:T(128)} %bitcast.me_ref.group_ref, f32[256,256]{1,0:T(8,128)S(1)} %get-tuple-element.29.refs_0_, bf16[256,256]{1,0:T(8,128)(2,1)S(1)} %collective-permute-done.10.refs_1_, ...), custom_call_target="tpu_custom_call" | custom-call | tf_op jit(solution)/shard_map/pallas_call | solution.py:130
  (75 shorter events, 24.8 us)
Async XLA Ops:
  2.6 29.9 %collective-permute-start.1 = (bf16[272,256]{1,0:T(8,128)(2,1)}, bf16[272,256]{1,0:T(8,128)(2,1)}, u32[]{:S(2)}, u32[]{:S(2)}) collective-permute-start(bf16[272,256]{1,0:T(8,128)(2,1)} %get-tuple-element.26), channel_id=1, source_target_pairs={{0,4},{2,6},{4,0},{6,2},{8,12},{10,14},{12,8},{14,10},{16,20},{18,... | collective-permute-start | bytes 417800 | tf_op jit(solution)/shard_map/ppermute | solution.py:371
  3.1 31.9 %collective-permute-start.2 = (bf16[272,256]{1,0:T(8,128)(2,1)}, bf16[272,256]{1,0:T(8,128)(2,1)}, u32[]{:S(2)}, u32[]{:S(2)}) collective-permute-start(bf16[272,256]{1,0:T(8,128)(2,1)} %get-tuple-element.27), channel_id=1, source_target_pairs={{0,6},{2,4},{4,2},{6,0},{8,14},{10,12},{12,10},{14,8},{16,22},{18,... | collective-permute-start | bytes 417800 | tf_op jit(solution)/shard_map/ppermute | solution.py:371
  4.6 34.9 %collective-permute-start = (bf16[272,256]{1,0:T(8,128)(2,1)}, bf16[272,256]{1,0:T(8,128)(2,1)}, u32[]{:S(2)}, u32[]{:S(2)}) collective-permute-start(bf16[272,256]{1,0:T(8,128)(2,1)} %get-tuple-element.25), channel_id=1, source_target_pairs={{0,2},{2,0},{4,6},{6,4},{8,10},{10,8},{12,14},{14,12},{16,18},{18,... | collective-permute-start | bytes 417800 | tf_op jit(solution)/shard_map/ppermute | solution.py:371
  8.5 53.9 %collective-permute-start.8 = (bf16[2,264,1024]{2,1,0:T(8,128)(2,1)}, bf16[2,264,1024]{2,1,0:T(8,128)(2,1)}, u32[]{:S(2)}, u32[]{:S(2)}) collective-permute-start(bf16[2,264,1024]{2,1,0:T(8,128)(2,1)} %shard_map.106), channel_id=1, source_target_pairs={{0,2},{2,0},{4,6},{6,4},{8,10},{10,8},{12,14},{14,12},{16,18},{18,... | collective-permute-start | bytes 3244040 | tf_op jit(solution)/shard_map/ppermute | solution.py:371
  11.5 51.0 %collective-permute-start.9 = (bf16[2,264,1024]{2,1,0:T(8,128)(2,1)}, bf16[2,264,1024]{2,1,0:T(8,128)(2,1)}, u32[]{:S(2)}, u32[]{:S(2)}) collective-permute-start(bf16[2,264,1024]{2,1,0:T(8,128)(2,1)} %shard_map.107), channel_id=1, source_target_pairs={{0,4},{2,6},{4,0},{6,2},{8,12},{10,14},{12,8},{14,10},{16,20},{18,... | collective-permute-start | bytes 3244040 | tf_op jit(solution)/shard_map/ppermute | solution.py:371
  12.7 0.5 copy-start.8
  13.3 6.5 %copy-start.7 = (s32[1024]{0:T(1024)}, s32[1024]{0:T(1024)S(1)}, u32[]{:S(2)}) copy-start(s32[1024]{0:T(1024)S(1)} %pad_clamp_fusion) | copy-start | bytes 12292
  22.8 0.7 copy-start.4
  23.5 2.2 %copy-start.5 = (s32[32]{0:T(128)S(1)}, s32[32]{0:T(128)}, u32[]{:S(2)}) copy-start(s32[32]{0:T(128)} %get-tuple-element.45) | copy-start | bytes 388
  23.5 4.7 %copy-start.6 = (s32[4,2]{1,0:T(4,128)S(1)}, s32[4,2]{1,0:T(4,128)}, u32[]{:S(2)}) copy-start(s32[4,2]{1,0:T(4,128)} %get-tuple-element.49) | copy-start | bytes 100
  32.5 49.5 %collective-permute-start.3 = (bf16[2,264,1024]{2,1,0:T(8,128)(2,1)}, bf16[2,264,1024]{2,1,0:T(8,128)(2,1)S(1)}, u32[]{:S(2)}, u32[]{:S(2)}) collective-permute-start(bf16[2,264,1024]{2,1,0:T(8,128)(2,1)} %shard_map.104), channel_id=1, source_target_pairs={{0,6},{2,4},{4,2},{6,0},{8,14},{10,12},{12,10},{14,8},{16,22},{18,... | collective-permute-start | bytes 3244040 | tf_op jit(solution)/shard_map/ppermute | solution.py:371
  35.9 10.7 %collective-permute-start.6 = (bf16[544,256]{1,0:T(8,128)(2,1)S(1)}, bf16[544,256]{1,0:T(8,128)(2,1)S(1)}, u32[]{:S(2)}, u32[]{:S(2)}) collective-permute-start(bf16[544,256]{1,0:T(8,128)(2,1)S(1)} %pad_maximum_fusion.1), channel_id=1, source_target_pairs={{0,8},{2,10},{4,12},{6,14},{8,16},{10,18},{12,20},{14,22},{16,24},... | collective-permute-start | bytes 835592 | tf_op jit(solution)/shard_map/ppermute | solution.py:375
  40.4 11.8 %collective-permute-start.4 = (bf16[544,256]{1,0:T(8,128)(2,1)S(1)}, bf16[544,256]{1,0:T(8,128)(2,1)S(1)}, u32[]{:S(2)}, u32[]{:S(2)}) collective-permute-start(bf16[544,256]{1,0:T(8,128)(2,1)S(1)} %pad_maximum_fusion), channel_id=1, source_target_pairs={{0,8},{2,10},{4,12},{6,14},{8,16},{10,18},{12,20},{14,22},{16,24},... | collective-permute-start | bytes 835592 | tf_op jit(solution)/shard_map/ppermute | solution.py:375
  46.7 11.5 %collective-permute-start.7 = (bf16[544,256]{1,0:T(8,128)(2,1)S(1)}, bf16[544,256]{1,0:T(8,128)(2,1)S(1)}, u32[]{:S(2)}, u32[]{:S(2)}) collective-permute-start(bf16[544,256]{1,0:T(8,128)(2,1)S(1)} %collective-permute-done.6.refs_9_.refs_7_), channel_id=1, source_target_pairs={{0,8},{2,10},{4,12},{6,14},{8,16},{10,18},{12,20},{14,22},{16,24},... | collective-permute-start | bytes 835592 | tf_op jit(solution)/shard_map/ppermute | solution.py:375
  52.3 10.2 %collective-permute-start.5 = (bf16[544,256]{1,0:T(8,128)(2,1)S(1)}, bf16[544,256]{1,0:T(8,128)(2,1)S(1)}, u32[]{:S(2)}, u32[]{:S(2)}) collective-permute-start(bf16[544,256]{1,0:T(8,128)(2,1)S(1)} %collective-permute-done.4.refs_8_.refs_6_), channel_id=1, source_target_pairs={{0,8},{2,10},{4,12},{6,14},{8,16},{10,18},{12,20},{14,22},{16,24},... | collective-permute-start | bytes 835592 | tf_op jit(solution)/shard_map/ppermute | solution.py:375
  62.5 1.2 copy-start
  63.7 0.9 copy-start.1
  64.6 0.7 copy-start.2
  65.3 16.8 %copy-start.3 = (s32[2,128]{1,0:T(2,128)S(1)}, s32[2,128]{1,0:T(2,128)}, u32[]{:S(2)}) copy-start(s32[2,128]{1,0:T(2,128)} %slice.44.refs_3_) | copy-start | bytes 3076
  90.1 17.9 %collective-permute-start.16 = (bf16[512,256]{1,0:T(8,128)(2,1)S(1)}, bf16[512,256]{1,0:T(8,128)(2,1)S(1)}, u32[]{:S(2)}, u32[]{:S(2)}) collective-permute-start(bf16[512,256]{1,0:T(8,128)(2,1)S(1)} %get-tuple-element.38), channel_id=1, source_target_pairs={{8,0},{10,2},{12,4},{14,6},{16,8},{18,10},{20,12},{22,14},{24,16},... | collective-permute-start | bytes 786440 | tf_op jit(solution)/shard_map/ppermute | solution.py:375
  92.0 5.6 %collective-permute-start.10 = (bf16[256,256]{1,0:T(8,128)(2,1)S(1)}, bf16[256,256]{1,0:T(8,128)(2,1)S(1)}, u32[]{:S(2)}, u32[]{:S(2)}) collective-permute-start(bf16[256,256]{1,0:T(8,128)(2,1)S(1)} %get-tuple-element.30), channel_id=1, source_target_pairs={{0,2},{2,0},{4,6},{6,4},{8,10},{10,8},{12,14},{14,12},{16,18},{18,... | collective-permute-start | bytes 393224 | tf_op jit(solution)/shard_map/ppermute | solution.py:371
  92.7 15.3 %collective-permute-start.11 = (bf16[256,256]{1,0:T(8,128)(2,1)S(1)}, bf16[256,256]{1,0:T(8,128)(2,1)S(1)}, u32[]{:S(2)}, u32[]{:S(2)}) collective-permute-start(bf16[256,256]{1,0:T(8,128)(2,1)S(1)} %get-tuple-element.31), channel_id=1, source_target_pairs={{0,4},{2,6},{4,0},{6,2},{8,12},{10,14},{12,8},{14,10},{16,20},{18,... | collective-permute-start | bytes 393224 | tf_op jit(solution)/shard_map/ppermute | solution.py:371
  93.1 31.2 %collective-permute-start.13 = (bf16[512,256]{1,0:T(8,128)(2,1)S(1)}, bf16[512,256]{1,0:T(8,128)(2,1)S(1)}, u32[]{:S(2)}, u32[]{:S(2)}) collective-permute-start(bf16[512,256]{1,0:T(8,128)(2,1)S(1)} %get-tuple-element.34), channel_id=1, source_target_pairs={{8,0},{10,2},{12,4},{14,6},{16,8},{18,10},{20,12},{22,14},{24,16},... | collective-permute-start | bytes 786440 | tf_op jit(solution)/shard_map/ppermute | solution.py:375
  95.1 47.5 %collective-permute-start.21 = (bf16[256,1024]{1,0:T(8,128)(2,1)S(1)}, bf16[256,1024]{1,0:T(8,128)(2,1)S(1)}, u32[]{:S(2)}, u32[]{:S(2)}) collective-permute-start(bf16[256,1024]{1,0:T(8,128)(2,1)S(1)} %get-tuple-element.44), channel_id=1, source_target_pairs={{0,6},{2,4},{4,2},{6,0},{8,14},{10,12},{12,10},{14,8},{16,22},{18,... | collective-permute-start | bytes 1572872 | tf_op jit(solution)/shard_map/ppermute | solution.py:371
  97.6 44.9 %collective-permute-start.19 = (bf16[256,1024]{1,0:T(8,128)(2,1)S(1)}, bf16[256,1024]{1,0:T(8,128)(2,1)S(1)}, u32[]{:S(2)}, u32[]{:S(2)}) collective-permute-start(bf16[256,1024]{1,0:T(8,128)(2,1)S(1)} %get-tuple-element.42), channel_id=1, source_target_pairs={{0,2},{2,0},{4,6},{6,4},{8,10},{10,8},{12,14},{14,12},{16,18},{18,... | collective-permute-start | bytes 1572872 | tf_op jit(solution)/shard_map/ppermute | solution.py:371
  107.9 34.6 %collective-permute-start.20 = (bf16[256,1024]{1,0:T(8,128)(2,1)S(1)}, bf16[256,1024]{1,0:T(8,128)(2,1)S(1)}, u32[]{:S(2)}, u32[]{:S(2)}) collective-permute-start(bf16[256,1024]{1,0:T(8,128)(2,1)S(1)} %get-tuple-element.43), channel_id=1, source_target_pairs={{0,4},{2,6},{4,0},{6,2},{8,12},{10,14},{12,8},{14,10},{16,20},{18,... | collective-permute-start | bytes 1572872 | tf_op jit(solution)/shard_map/ppermute | solution.py:371
  107.9 14.5 %collective-permute-start.12 = (bf16[256,256]{1,0:T(8,128)(2,1)S(1)}, bf16[256,256]{1,0:T(8,128)(2,1)S(1)}, u32[]{:S(2)}, u32[]{:S(2)}) collective-permute-start(bf16[256,256]{1,0:T(8,128)(2,1)S(1)} %get-tuple-element.32), channel_id=1, source_target_pairs={{0,6},{2,4},{4,2},{6,0},{8,14},{10,12},{12,10},{14,8},{16,22},{18,... | collective-permute-start | bytes 393224 | tf_op jit(solution)/shard_map/ppermute | solution.py:371
  122.4 8.2 %collective-permute-start.17 = (bf16[256,256]{1,0:T(8,128)(2,1)S(1)}, bf16[256,256]{1,0:T(8,128)(2,1)S(1)}, u32[]{:S(2)}, u32[]{:S(2)}) collective-permute-start(bf16[256,256]{1,0:T(8,128)(2,1)S(1)} %get-tuple-element.39), channel_id=1, source_target_pairs={{8,4},{10,6},{12,0},{14,2},{16,12},{18,14},{20,8},{22,10},{24,20},... | collective-permute-start | bytes 393224 | tf_op jit(solution)/shard_map/ppermute | solution.py:438
  124.4 8.7 %collective-permute-start.18 = (bf16[256,256]{1,0:T(8,128)(2,1)S(1)}, bf16[256,256]{1,0:T(8,128)(2,1)S(1)}, u32[]{:S(2)}, u32[]{:S(2)}) collective-permute-start(bf16[256,256]{1,0:T(8,128)(2,1)S(1)} %get-tuple-element.40), channel_id=1, source_target_pairs={{8,6},{10,4},{12,2},{14,0},{16,14},{18,12},{20,10},{22,8},{24,22},... | collective-permute-start | bytes 393224 | tf_op jit(solution)/shard_map/ppermute | solution.py:438
  130.7 8.8 %collective-permute-start.14 = (bf16[256,256]{1,0:T(8,128)(2,1)S(1)}, bf16[256,256]{1,0:T(8,128)(2,1)S(1)}, u32[]{:S(2)}, u32[]{:S(2)}) collective-permute-start(bf16[256,256]{1,0:T(8,128)(2,1)S(1)} %get-tuple-element.35), channel_id=1, source_target_pairs={{8,0},{10,2},{12,4},{14,6},{16,8},{18,10},{20,12},{22,14},{24,16},... | collective-permute-start | bytes 393224 | tf_op jit(solution)/shard_map/ppermute | solution.py:438
  133.0 9.5 %collective-permute-start.15 = (bf16[256,256]{1,0:T(8,128)(2,1)S(1)}, bf16[256,256]{1,0:T(8,128)(2,1)S(1)}, u32[]{:S(2)}, u32[]{:S(2)}) collective-permute-start(bf16[256,256]{1,0:T(8,128)(2,1)S(1)} %get-tuple-element.36), channel_id=1, source_target_pairs={{8,2},{10,0},{12,6},{14,4},{16,10},{18,8},{20,14},{22,12},{24,18},... | collective-permute-start | bytes 393224 | tf_op jit(solution)/shard_map/ppermute | solution.py:438
